TPU v7x, 768 devices: a whole 4x8x12 slice. The times are simulated.
768 devices in a mesh: gx: 96 (over z, x, core), gy: 8 (over y).
Axes of the slice: x: 4, y: 8, z: 12, core: 2. Of those that a mesh axis runs over, the one named last changes fastest.
Arguments:
- fields: float32 [4, 192, 8, 16, 8, 128], P(None, 'gx', None, 'gy'), may hold values from -6 to 6
- viscosity: float32 [192, 8, 16, 8, 128], P('gx', None, 'gy'), may hold values from 0.002 to 0.02
- inv_density: float32 [192, 16, 16], P('gx', 'gy'), may hold values from 0.5 to 2
- elem_group: int32 [192, 16, 16], P('gx', 'gy'), may hold values from 0 to 3
- coarse_inverse: float32 [3072, 3072], P(('gx', 'gy')), as said below
Outputs:
- fields_new: float32 [4, 192, 8, 16, 8, 128], P(None, 'gx', None, 'gy')
- pressure: float32 [192, 8, 16, 8, 128], P('gx', None, 'gy')
Inputs may be any that keep to these rules, and one draw needn't show every extreme that they name: `elem_group`: the coarse unknown of an element among the 4 of its own device. `coarse_inverse`: symmetric and positive definite.
All inputs are finite; a program needn't handle non-finite values.
Results may differ from a plain program's by a relative error of at most 0.0015.
Values sent between devices are 32-bit elements; how exact they have to be, the bound alone decides.
A program may use at most 32 MiB of HBM per device.

v0:
```python
import jax
import jax.numpy as jnp
import numpy as np
from jax import lax
from jax.sharding import PartitionSpec as P

ORDER = 7
ITERS = 2
NCD = 4


dt_step = 0.01
sigma_p = 4.0
prandtl = 0.7
cheb_ratio = 0.1


def with_halo(cells, sides, width):
    for axis, dim in sides:
        count = lax.axis_size(axis)
        ends = count - 1
        head = lax.slice_in_dim(cells, 0, width, axis=dim)
        tail = lax.slice_in_dim(cells, cells.shape[dim] - width, cells.shape[dim], axis=dim)
        cells = jnp.concatenate(
            [
                lax.ppermute(tail, axis, [(i, (i + 1) % count) for i in range(ends)]),
                cells,
                lax.ppermute(head, axis, [((i + 1) % count, i) for i in range(ends)]),
            ],
            axis=dim,
        )
    return cells


def tables():
    points = np.array(
        [
            -1.0,
            -0.8717401485096066,
            -0.5917001814331423,
            -0.2092992179024789,
            0.2092992179024789,
            0.5917001814331423,
            0.8717401485096066,
            1.0,
        ]
    )
    weights = np.array(
        [
            1.0 / 28.0,
            0.2107042271435061,
            0.3411226924835044,
            0.4124587946587038,
            0.4124587946587038,
            0.3411226924835044,
            0.2107042271435061,
            1.0 / 28.0,
        ]
    )
    identity = np.eye(8)
    differ = points[:, None] - points[None, :] + identity
    barycentric = 1.0 / np.prod(differ, axis=1)
    offdiag = barycentric[None, :] / barycentric[:, None] / differ * (1.0 - identity)
    derivative = offdiag - identity * np.sum(offdiag, axis=1)[:, None]
    mass_one = identity * weights[None, :]
    stiff_one = derivative.T @ mass_one @ derivative
    stiff_three = (
        np.kron(np.kron(stiff_one, mass_one), mass_one)
        + np.kron(np.kron(mass_one, stiff_one), mass_one)
        + np.kron(np.kron(mass_one, mass_one), stiff_one)
    )
    three_diag = np.sum(stiff_three * np.eye(512), axis=1)
    spectral_bound = float(np.max(np.sum(np.abs(stiff_three), axis=1) / three_diag))
    return (derivative, weights, np.sum(stiff_one * identity, axis=1), spectral_bound)


def join_pairs(field, elem_axis):
    node_axis = elem_axis + 1
    top_node = field.shape[node_axis] - 1
    last_face = lax.index_in_dim(field, top_node, node_axis, keepdims=False)
    first_face = lax.index_in_dim(field, 0, node_axis, keepdims=False)
    elem_count = field.shape[elem_axis]
    summed = lax.slice_in_dim(last_face, 0, elem_count - 1, axis=elem_axis) + lax.slice_in_dim(
        first_face, 1, elem_count, axis=elem_axis
    )
    new_last = jnp.concatenate(
        [summed, lax.slice_in_dim(last_face, elem_count - 1, elem_count, axis=elem_axis)], elem_axis
    )
    new_first = jnp.concatenate(
        [lax.slice_in_dim(first_face, 0, 1, axis=elem_axis), summed], elem_axis
    )
    middle = lax.slice_in_dim(field, 1, top_node, axis=node_axis)
    return jnp.concatenate(
        [jnp.expand_dims(new_first, node_axis), middle, jnp.expand_dims(new_last, node_axis)],
        node_axis,
    )


def add_edges(grid, extra_first, extra_last, edge_dim):
    extent = grid.shape[edge_dim]
    return jnp.concatenate(
        [
            lax.slice_in_dim(grid, 0, 1, axis=edge_dim) + extra_first,
            lax.slice_in_dim(grid, 1, extent - 1, axis=edge_dim),
            lax.slice_in_dim(grid, extent - 1, extent, axis=edge_dim) + extra_last,
        ],
        edge_dim,
    )


def per_device(fields, viscosity, inv_density, elem_group, coarse_inverse):
    precision = lax.Precision.HIGHEST
    derivative_np, weights_np, stiff_np, spectral_bound = tables()
    line_nodes = ORDER + 1
    elems_x = fields.shape[1]
    elems_y = fields.shape[3]
    length = fields.shape[5]
    elems_z = length // line_nodes
    rows_x = elems_x * line_nodes
    rows_y = elems_y * line_nodes
    derivative = jnp.asarray(derivative_np, jnp.float32)
    weights_line = jnp.asarray(weights_np, jnp.float32)
    stiff_line = jnp.asarray(stiff_np, jnp.float32)
    band_np = np.kron(np.eye(elems_z), derivative_np)
    band_matrix = jnp.asarray(band_np, jnp.float32)
    band_trans = jnp.asarray(band_np.T, jnp.float32)
    pair_np = np.eye(length)
    joints = np.arange(elems_z - 1) * line_nodes + ORDER
    pair_np[joints, joints + 1] = 1.0
    pair_np[joints + 1, joints] = 1.0
    pair_table = jnp.asarray(pair_np, jnp.float32)
    block_np = np.kron(np.eye(elems_z), np.ones((line_nodes, 1)))
    block_table = jnp.asarray(block_np, jnp.float32)
    block_trans = jnp.asarray(block_np.T, jnp.float32)

    def gradient(field):
        along_x = jnp.einsum("ia,cxaybl->cxiybl", derivative, field, precision=precision)
        along_y = jnp.einsum("jb,cxaybl->cxayjl", derivative, field, precision=precision)
        along_z = jnp.matmul(field, band_trans, precision=precision)
        return (along_x, along_y, along_z)

    def adjoint(first_part, second_part, third_part):
        result = jnp.einsum("ai,cxaybl->cxiybl", derivative, first_part, precision=precision)
        result = result + jnp.einsum(
            "bj,cxaybl->cxayjl", derivative, second_part, precision=precision
        )
        return result + jnp.matmul(third_part, band_matrix, precision=precision)

    def assemble(field):
        channels = field.shape[0]
        field = join_pairs(field, 1)
        grid = field.reshape(channels, rows_x, rows_y, length)
        border = with_halo(grid, (("gx", 1),), 1)
        grid = add_edges(grid, border[:, 0:1], border[:, -1:], 1)
        field = join_pairs(
            grid.reshape(channels, elems_x, line_nodes, elems_y, line_nodes, length), 3
        )
        grid = field.reshape(channels, rows_x, rows_y, length)
        border = with_halo(grid, (("gy", 2),), 1)
        grid = add_edges(grid, border[:, :, 0:1], border[:, :, -1:], 2)
        field = grid.reshape(channels, elems_x, line_nodes, elems_y, line_nodes, length)
        return jnp.matmul(field, pair_table, precision=precision)

    def on_x(values):
        return values[None, :, None, None, None]

    def on_y(values):
        return values[None, None, None, :, None]

    weights_z = jnp.tile(weights_line, elems_z)
    stiff_z = jnp.tile(stiff_line, elems_z)
    weight = on_x(weights_line) * on_y(weights_line) * weights_z
    diag_stiff = (
        on_x(stiff_line) * on_y(weights_line) * weights_z
        + on_x(weights_line) * on_y(stiff_line) * weights_z
        + on_x(weights_line) * on_y(weights_line) * stiff_z
    )
    kappa = jnp.dot(inv_density, block_trans, precision=precision)[:, None, :, None, :]
    unit = jnp.ones((1, elems_x, line_nodes, elems_y, line_nodes, length), jnp.float32)
    stacked = jnp.concatenate(
        [unit, unit * weight, (kappa * diag_stiff + sigma_p * weight)[None], fields * weight], 0
    )
    summed = assemble(stacked)
    multiplicity = summed[0]
    mass_sum = summed[1]
    pdiag = summed[2]
    start = summed[3:] / mass_sum
    along_x, along_y, along_z = gradient(start)
    advect = start[0] * along_x + start[1] * along_y + start[2] * along_z
    factors = jnp.asarray([1.0, 1.0, 1.0, 1.0 / prandtl], jnp.float32)[
        :, None, None, None, None, None
    ]
    scaled = factors * viscosity * weight
    rhs = -weight * advect - adjoint(scaled * along_x, scaled * along_y, scaled * along_z)
    fields_new = start + dt_step * assemble(rhs) / mass_sum
    div_x = jnp.einsum("ia,xaybl->xiybl", derivative, fields_new[0], precision=precision)
    div_y = jnp.einsum("jb,xaybl->xayjl", derivative, fields_new[1], precision=precision)
    div_z = jnp.matmul(fields_new[2], band_trans, precision=precision)
    rhs_p = assemble((-weight * (div_x + div_y + div_z))[None])[0]
    inv_mult = 1.0 / multiplicity
    inv_diag = 1.0 / pdiag
    kappa_weight = kappa * weight
    one_hot = (elem_group[..., None] == jnp.arange(NCD, dtype=jnp.int32)).astype(jnp.float32)

    def op_local(field):
        grad_x, grad_y, grad_z = gradient(field[None])
        return (
            adjoint(kappa_weight * grad_x, kappa_weight * grad_y, kappa_weight * grad_z)[0]
            + sigma_p * weight * field
        )

    def restrict(resid):
        node_sums = (resid * inv_mult).sum(axis=(1, 3))
        elem_sums = jnp.dot(node_sums, block_table, precision=precision)
        return jnp.einsum("xyz,xyzk->k", elem_sums, one_hot, precision=precision)

    def gather_rest(resid):
        return lax.all_gather(restrict(resid), ("gx", "gy"), axis=0, tiled=True)

    def total(value):
        return lax.psum(value, ("gx", "gy"))

    lower = cheb_ratio * spectral_bound
    cheb_theta = 0.5 * (spectral_bound + lower)
    cheb_delta = 0.5 * (spectral_bound - lower)

    def precondition(resid, restricted_all):
        coarse_values = jnp.dot(coarse_inverse, restricted_all, precision=precision)
        elem_values = jnp.einsum("xyzk,k->xyz", one_hot, coarse_values, precision=precision)
        spread = jnp.dot(elem_values, block_trans, precision=precision)[:, None, :, None, :]
        coarse_local = spread * inv_mult
        update = resid * inv_diag / cheb_theta
        smoothed = update
        cheb_rho = cheb_delta / cheb_theta
        local = op_local(smoothed)
        both = assemble(jnp.stack([local, coarse_local], 0))
        applied = both[0]
        coarse_term = both[1]
        defect = resid - applied
        rho_next = 1.0 / (2.0 * cheb_theta / cheb_delta - cheb_rho)
        update = rho_next * cheb_rho * update + 2.0 * rho_next / cheb_delta * defect * inv_diag
        smoothed = smoothed + update
        return smoothed + coarse_term

    pressure = jnp.zeros_like(rhs_p)
    resid = rhs_p
    restricted_all = gather_rest(resid)
    precond_r = precondition(resid, restricted_all)
    rz_value = total(jnp.sum(resid * precond_r * inv_mult))
    direction = precond_r
    for iteration in range(ITERS):
        last_turn = iteration + 1 == ITERS
        image = assemble(op_local(direction)[None])[0]
        partial_sum = jnp.sum(direction * image * inv_mult)
        curvature = total(partial_sum)
        step_size = rz_value / curvature
        pressure = pressure + step_size * direction
        if not last_turn:
            resid = resid - step_size * image
            restricted_all = gather_rest(resid)
            precond_r = precondition(resid, restricted_all)
            rz_next = total(jnp.sum(resid * precond_r * inv_mult))
            direction = precond_r + rz_next / rz_value * direction
            rz_value = rz_next
    return (fields_new, pressure)


def solution(mesh):
    placed = (
        P(None, "gx", None, "gy", None, None),
        P("gx", None, "gy", None, None),
        P("gx", "gy", None),
        P("gx", "gy", None),
        P(("gx", "gy"), None),
    )
    return jax.shard_map(
        per_device,
        mesh=mesh,
        in_specs=placed,
        out_specs=(P(None, "gx", None, "gy", None, None), P("gx", None, "gy", None, None)),
        check_vma=False,
    )
```

profile of v0, /device:TPU:1, one launch (start us, length us, event | category | flops | bytes accessed | tf_op | source)
XLA Modules:
  0.0 725.4 jit_solution(3846485880295587315)
XLA Ops:
  3.1 1.2 copy_multiply_fusion
  5.4 4.5 collective-permute-start
  9.9 9.2 %collective-permute-start.1 = (f32[7,1,16,128]{3,2,1,0:T(8,128)S(1)}, f32[7,1,16,128]{3,2,1,0:T(8,128)S(1)}, u32[]{:S(2)}, u32[]{:S(2)}) collective-permute-start(f32[7,1,16,128]{3,2,1,0:T(8,128)S(1)} %get-tuple-element.19), channel_id=1, source_target_pairs={{8,0},{16,8},{24,16},{32,24},{40,32},{48,40},{56,48},{64,56},{72,6... | collective-permute-start | bytes 172040 | tf_op jit(solution)/shard_map/ppermute | solution.py:28
  21.1 1.3 collective-permute-start.2
  22.4 1.3 collective-permute-start.3
  23.9 3.4 collective-permute-done.3
  34.5 1.0 fusion.2
  36.0 1.9 collective-permute-start.4
  38.0 2.8 collective-permute-start.5
  40.8 2.4 collective-permute-done.5
  43.9 2.2 collective-permute-start.6
  46.1 1.5 collective-permute-start.7
  47.6 3.4 collective-permute-done.7
  54.1 3.1 collective-permute-start.8
  57.2 1.9 collective-permute-start.9
  59.1 3.0 collective-permute-done.9
  62.4 5.2 collective-permute-start.10
  67.6 1.3 collective-permute-start.11
  68.9 3.3 collective-permute-done.11
  76.1 124.3 %all-reduce = f32[3072]{0:T(1024)S(1)} all-reduce(f32[3072]{0:T(1024)S(1)} %dynamic-update-slice), channel_id=1, replica_groups=mesh['gx'=96,'gy'=8] {'gx','gy'}, use_global_device_ids=true, to_apply=%add | all-reduce | flops 3072 | bytes 24576
  202.8 2.2 collective-permute-start.12
  205.0 2.1 collective-permute-start.13
  207.2 2.9 collective-permute-done.13
  210.4 1.3 collective-permute-start.14
  211.7 1.3 collective-permute-start.15
  213.1 3.1 collective-permute-done.15
  220.1 3.1 collective-permute-start.16
  223.3 1.9 collective-permute-start.17
  225.2 3.0 collective-permute-done.17
  228.5 4.0 collective-permute-start.18
  232.5 1.3 collective-permute-start.19
  233.8 4.9 collective-permute-done.19
  239.8 113.5 %all-reduce.2 = (f32[]{:T(128)}, f32[]{:T(128)}) all-reduce(f32[]{:T(128)} %get-tuple-element.3, f32[]{:T(128)} %get-tuple-element.2), channel_id=1, replica_groups=mesh['gx'=96,'gy'=8] {'gx','gy'}, use_global_device_ids=true, to_apply=%region_2.0 | all-reduce | flops 2 | bytes 16 | tf_op jit(solution)/shard_map/psum | solution.py:221
  356.5 103.7 %all-reduce.1 = f32[3072]{0:T(1024)S(1)} all-reduce(f32[3072]{0:T(1024)S(1)} %dynamic-update-slice.1), channel_id=1, replica_groups=mesh['gx'=96,'gy'=8] {'gx','gy'}, use_global_device_ids=true, to_apply=%add.1 | all-reduce | flops 3072 | bytes 24576
  461.7 4.2 collective-permute-start.20
  466.0 1.9 collective-permute-start.21
  467.9 3.1 collective-permute-done.21
  471.4 1.3 collective-permute-start.22
  472.7 1.5 collective-permute-start.23
  474.3 4.4 collective-permute-done.23
  479.8 109.1 %psum.30 = f32[]{:T(128)} all-reduce(f32[]{:T(128)} %fusion.82), channel_id=1, replica_groups=mesh['gx'=96,'gy'=8] {'gx','gy'}, use_global_device_ids=true, to_apply=%region_7.0 | all-reduce | flops 1 | bytes 8 | tf_op jit(solution)/shard_map/psum | solution.py:221
  593.6 2.2 collective-permute-start.24
  595.8 2.1 collective-permute-start.25
  597.9 2.8 collective-permute-done.25
  601.0 4.1 collective-permute-start.26
  605.1 1.3 collective-permute-start.27
  606.4 4.8 collective-permute-done.27
  612.1 111.3 %psum.31 = f32[]{:T(128)} all-reduce(f32[]{:T(128)} %fusion.37), channel_id=1, replica_groups=mesh['gx'=96,'gy'=8] {'gx','gy'}, use_global_device_ids=true, to_apply=%region_9.0 | all-reduce | flops 1 | bytes 8 | tf_op jit(solution)/shard_map/psum | solution.py:221
  (273 shorter events, 38.2 us)
Async XLA Ops:
  0.6 199.8 %copy-start = (f32[4,3072]{1,0:T(4,128)S(1)}, f32[4,3072]{1,0:T(4,128)}, u32[]{:S(2)}) copy-start(f32[4,3072]{1,0:T(4,128)} %param.18) | copy-start | bytes 147460
  0.6 0.7 copy-start.16
  2.3 0.7 copy-start.10
  2.3 0.7 copy-start.18
  5.4 13.8 %collective-permute-start = (f32[7,1,16,128]{3,2,1,0:T(8,128)S(1)}, f32[7,1,16,128]{3,2,1,0:T(8,128)S(1)}, u32[]{:S(2)}, u32[]{:S(2)}) collective-permute-start(f32[7,1,16,128]{3,2,1,0:T(8,128)S(1)} %get-tuple-element.18), channel_id=1, source_target_pairs={{0,8},{8,16},{16,24},{24,32},{32,40},{40,48},{48,56},{56,64},{64,7... | collective-permute-start | bytes 172040 | tf_op jit(solution)/shard_map/ppermute | solution.py:26
  9.9 10.1 %collective-permute-start.1 = (f32[7,1,16,128]{3,2,1,0:T(8,128)S(1)}, f32[7,1,16,128]{3,2,1,0:T(8,128)S(1)}, u32[]{:S(2)}, u32[]{:S(2)}) collective-permute-start(f32[7,1,16,128]{3,2,1,0:T(8,128)S(1)} %get-tuple-element.19), channel_id=1, source_target_pairs={{8,0},{16,8},{24,16},{32,24},{40,32},{48,40},{56,48},{64,56},{72,6... | collective-permute-start | bytes 172040 | tf_op jit(solution)/shard_map/ppermute | solution.py:28
  21.0 2.7 copy-start.9
  21.1 2.8 collective-permute-start.2
  22.4 4.9 collective-permute-start.3
  27.5 0.8 copy-start.4
  29.3 0.7 copy-start.11
  31.3 0.8 copy-start.13
  33.0 0.8 copy-start.12
  36.0 4.8 collective-permute-start.4
  38.0 5.2 collective-permute-start.5
  43.9 3.8 collective-permute-start.6
  46.1 5.0 collective-permute-start.7
  51.8 1.3 copy-start.7
  51.9 0.7 copy-start.1
  52.8 0.8 copy-start.3
  54.1 5.0 collective-permute-start.8
  57.2 5.0 collective-permute-start.9
  62.4 6.5 collective-permute-start.10
  67.6 4.7 collective-permute-start.11
  72.3 0.8 copy-start.14
  74.2 0.8 copy-start.8
  75.0 0.7 copy-start.19
  201.2 0.8 copy-start.2
  202.8 4.4 collective-permute-start.12
  205.0 5.1 collective-permute-start.13
  210.4 2.6 collective-permute-start.14
  211.7 4.5 collective-permute-start.15
  218.6 0.7 copy-start.6
  219.2 0.9 slice-start.1
  220.1 5.1 collective-permute-start.16
  223.3 5.0 collective-permute-start.17
  228.5 5.3 collective-permute-start.18
  232.5 6.3 collective-permute-start.19
  461.7 6.2 collective-permute-start.20
  466.0 5.1 collective-permute-start.21
  471.4 2.9 collective-permute-start.22
  472.7 5.9 collective-permute-start.23
  592.0 0.7 copy-start.5
  592.7 0.9 slice-start
  593.6 4.4 collective-permute-start.24
  595.8 5.0 collective-permute-start.25
  601.0 5.4 collective-permute-start.26
  605.1 6.1 collective-permute-start.27
  (2 other events, 1.3 us)
where the time goes:
time: 732 us; the launch traced here: 725 us
  blocking collectives  562 us (77%)
  starting transfers between devices  72.1 us (10%)
  waiting for transfers between devices  45.5 us (6%)
  matrix products  18.4 us (3%)
  local copies, waits for them, and re-layouts  14 us (2%)
    psum x3, blocking collectives, total(): return lax.psum(value, ('gx', 'gy'))  334 us
    unnamed x2, blocking collectives  228 us
    ppermute x14, waiting for transfers between devices, with_halo(): lax.ppermute(head, axis, [((i + 1) % count, i) for i in range(ends)])  45.5 us
    ppermute x14, starting transfers between devices, with_halo(): lax.ppermute(tail, axis, [(i, (i + 1) % count) for i in range(ends)])  40.6 us
    ppermute x14, starting transfers between devices, with_halo(): lax.ppermute(head, axis, [((i + 1) % count, i) for i in range(ends)])  31.4 us
  transfers between devices with their start and end apart: 28, of which 14 were waited for; matrix products, arithmetic and copies ran while one was open for 0% of the time, Pallas kernels for 0%

commit v1 on v0

v1 whole, which is shorter than its diff:
```python
import functools

import jax
import jax.numpy as jnp
import numpy as np
from jax import lax
from jax.experimental import pallas as pl
from jax.experimental.pallas import tpu as pltpu
from jax.sharding import PartitionSpec as P

NCD = 4
XC = 8
YL = 8

dt_step = 0.01
sigma_p = 4.0
prandtl = 0.7
cheb_ratio = 0.1

F32 = jnp.float32
BF16 = jnp.bfloat16
DIRS = [(-1, 0), (1, 0), (0, -1), (0, 1), (-1, -1), (-1, 1), (1, -1), (1, 1)]
MESH = pl.DeviceIdType.MESH


def tables():
    points = np.array(
        [
            -1.0,
            -0.8717401485096066,
            -0.5917001814331423,
            -0.2092992179024789,
            0.2092992179024789,
            0.5917001814331423,
            0.8717401485096066,
            1.0,
        ]
    )
    weights = np.array(
        [
            1.0 / 28.0,
            0.2107042271435061,
            0.3411226924835044,
            0.4124587946587038,
            0.4124587946587038,
            0.3411226924835044,
            0.2107042271435061,
            1.0 / 28.0,
        ]
    )
    identity = np.eye(8)
    differ = points[:, None] - points[None, :] + identity
    barycentric = 1.0 / np.prod(differ, axis=1)
    offdiag = barycentric[None, :] / barycentric[:, None] / differ * (1.0 - identity)
    derivative = offdiag - identity * np.sum(offdiag, axis=1)[:, None]
    mass_one = identity * weights[None, :]
    stiff_one = derivative.T @ mass_one @ derivative
    stiff_three = (
        np.kron(np.kron(stiff_one, mass_one), mass_one)
        + np.kron(np.kron(mass_one, stiff_one), mass_one)
        + np.kron(np.kron(mass_one, mass_one), stiff_one)
    )
    three_diag = np.sum(stiff_three * np.eye(512), axis=1)
    spectral_bound = float(np.max(np.sum(np.abs(stiff_three), axis=1) / three_diag))
    return derivative, weights, stiff_one, spectral_bound


DER, WTS, STF, SBOUND = tables()
KLN = np.diag(STF)


def constants():
    cols = np.stack([DER, DER.T, STF], 0)
    cy = np.broadcast_to(np.transpose(cols, (0, 2, 1))[:, :, :, None], (3, 8, 8, 128))

    def big(one):
        full = np.kron(np.eye(16), one).astype(np.float32)
        high = np.asarray(full, dtype=jnp.bfloat16)
        low = np.asarray(full - high.astype(np.float32), dtype=jnp.bfloat16)
        return np.block([[high, low], [high, np.zeros_like(low)]])

    bz = np.stack([big(DER.T), big(DER), big(STF)], 0)
    wy = np.tile(WTS, 2)[:, None]
    ky = np.tile(KLN, 2)[:, None]
    wz = np.tile(WTS, 16)[None, :]
    kz = np.tile(KLN, 16)[None, :]
    one = np.ones((16, 128))
    cp = np.stack([wy * wz, one * wz, wy * one, ky * wz + wy * kz, 1.0 / (wy * wz)], 0)
    spread = np.kron(np.eye(16), np.ones((1, 8)))
    return (
        jnp.asarray(np.ascontiguousarray(cy), F32),
        jnp.asarray(bz, BF16),
        jnp.asarray(cp, F32),
        jnp.asarray(spread, F32),
    )


def kernel(
    nx, ny, nxc,
    fields, visc, dens, grp, coarse, cy, bz, cp, spr,
    out_f, out_p,
    F, FN, V, L4, L1, W, IM, KAP, INVD, CX, AUX, AUXR, OH, PC,
    T1, T2, T3, R0, S0, Z0, W1, ZI,
    sx4, sy4, sc4, rx4, ry4, rc4, sx1, sy1, sc1, rx1, ry1, rc1,
    ag1, ag2, ag3,
    s_sem, r_sem, as_sem, ar_sem, cs_sem, cr_sem, gs_sem, gr_sem, l_sem,
):
    gx = lax.axis_index("gx")
    gy = lax.axis_index("gy")
    nz = nx // nxc
    xc = gx % nxc
    zc = gx // nxc

    def nbr(dx, dy):
        return ((gx + dx + nx) % nx, (gy + dy + ny) % ny)

    def y_mate(k):
        return (gx, (gy + k) % ny)

    def x_mate(k):
        return (zc * nxc + (xc + k) % nxc, gy)

    def z_mate(k):
        return (((zc + k) % nz) * nxc + xc, gy)

    mates = [nbr(dx, dy) for dx, dy in DIRS]
    mates += [y_mate(k) for k in range(1, ny)]
    mates += [x_mate(k) for k in range(1, nxc)]
    mates += [z_mate(k) for k in range(1, nz)]
    barrier = pltpu.get_barrier_semaphore()
    for mate in mates:
        pl.semaphore_signal(barrier, inc=1, device_id=mate, device_id_type=MESH)

    load_f = pltpu.make_async_copy(fields, F, l_sem.at[0])
    load_v = pltpu.make_async_copy(visc, V, l_sem.at[1])
    load_c = pltpu.make_async_copy(coarse, CX.at[8], l_sem.at[2])
    load_f.start()
    load_v.start()
    load_c.start()

    lane = lax.broadcasted_iota(jnp.int32, (8, 128), 1)
    sub = lax.broadcasted_iota(jnp.int32, (8, 128), 0)
    one = jnp.float32(1.0)
    zero = jnp.float32(0.0)
    j7 = jnp.where((lane % 8 == 7) & (lane < 127), one, zero)
    j0 = jnp.where((lane % 8 == 0) & (lane > 0), one, zero)
    j7p = jnp.concatenate([j7, j7], 0)
    j0p = jnp.concatenate([j0, j0], 0)
    s0 = jnp.where(sub == 0, one, zero)
    s7 = jnp.where(sub == 7, one, zero)

    has_l = jnp.where(gx > 0, one, zero)
    has_r = jnp.where(gx < nx - 1, one, zero)
    has_b = jnp.where(gy > 0, one, zero)
    has_t = jnp.where(gy < ny - 1, one, zero)
    vx = {-1: has_l, 0: one, 1: has_r}
    vy = {-1: has_b, 0: one, 1: has_t}

    def zjoin(v):
        return v + j7p * pltpu.roll(v, 127, 1) + j0p * pltpu.roll(v, 1, 1)

    def rows(x, base=0):
        return pl.ds(base + 16 * x, 16)

    def xyjoin(L, base=0):
        both = L[pl.ds(base + 112, 16), :] + L[pl.ds(base + 128, 16), :]
        L[pl.ds(base + 112, 16), :] = both
        L[pl.ds(base + 128, 16), :] = both
        pair = L[pl.ds(base + 7, 16, stride=16), :] + L[pl.ds(base + 8, 16, stride=16), :]
        L[pl.ds(base + 7, 16, stride=16), :] = pair
        L[pl.ds(base + 8, 16, stride=16), :] = pair

    def yop(plane, which):
        parts = []
        for t in range(2):
            tile = plane[8 * t : 8 * t + 8, :]
            total = None
            for b in range(8):
                term = jnp.broadcast_to(tile[b : b + 1, :], (8, 128)) * cy[which, b]
                total = term if total is None else total + term
            parts.append(total)
        return jnp.concatenate(parts, 0)

    def xop(planes, coef):
        total = None
        for a in range(8):
            term = planes[a] * jnp.float32(coef[a])
            total = term if total is None else total + term
        return total

    def zop(f, which):
        high = f.astype(BF16)
        low = (f - high.astype(F32)).astype(BF16)
        both = jnp.concatenate([high, low], 1)
        prod = jnp.dot(both, bz[which], preferred_element_type=F32)
        return prod[:, :128] + prod[:, 128:]

    def faces(L, nch, e, sx, sy, sc, rx, ry, rc, num):
        for c in range(nch):
            base = 256 * c
            sx[e, 0, pl.ds(16 * c, 16), :] = L[pl.ds(base, 16), :]
            sx[e, 1, pl.ds(16 * c, 16), :] = L[pl.ds(base + 240, 16), :]
            sy[e, 0, pl.ds(16 * c, 16), :] = L[pl.ds(base, 16, stride=16), :]
            sy[e, 1, pl.ds(16 * c, 16), :] = L[pl.ds(base + 15, 16, stride=16), :]
            for k, (dx, dy) in enumerate(DIRS[4:]):
                row = base + (240 if dx > 0 else 0) + (15 if dy > 0 else 0)
                sc[e, k, pl.ds(c, 1), :] = L[pl.ds(row, 1), :]
        copies = []
        for d in (4, 5, 6, 7, 0, 1, 2, 3):
            if d < 2:
                src, dst = sx.at[e, d], rx.at[e, d]
            elif d < 4:
                src, dst = sy.at[e, d - 2], ry.at[e, d - 2]
            else:
                src, dst = sc.at[e, d - 4], rc.at[e, d - 4]
            copy = pltpu.make_async_remote_copy(
                src, dst, s_sem.at[num, d], r_sem.at[num, d],
                device_id=nbr(*DIRS[d]), device_id_type=MESH,
            )
            copy.start()
            copies.append(copy)
        return copies

    def finish(copies, L, nch, e, rx, ry, rc):
        for copy in copies:
            copy.wait_recv()
        for c in range(nch):
            base = 256 * c
            at = pl.ds(16 * c, 16)
            lo, hi = pl.ds(base, 16), pl.ds(base + 240, 16)
            L[lo, :] = L[lo, :] + has_l * rx[e, 1, at, :]
            L[hi, :] = L[hi, :] + has_r * rx[e, 0, at, :]
            lo, hi = pl.ds(base, 16, stride=16), pl.ds(base + 15, 16, stride=16)
            L[lo, :] = L[lo, :] + has_b * ry[e, 1, at, :]
            L[hi, :] = L[hi, :] + has_t * ry[e, 0, at, :]
            for k, (dx, dy) in enumerate(DIRS[4:]):
                row = pl.ds(base + (0 if dx > 0 else 240) + (0 if dy > 0 else 15), 1)
                L[row, :] = L[row, :] + (vx[-dx] * vy[-dy]) * rc[e, k, pl.ds(c, 1), :]

    set4 = (sx4, sy4, sc4, rx4, ry4, rc4)
    set1 = (sx1, sy1, sc1, rx1, ry1, rc1)
    pending = []

    for ex in range(2):
        AUX[pl.ds(2 * ex, 2), :] = jnp.dot(
            dens[ex], spr[...], preferred_element_type=F32, precision=lax.Precision.HIGHEST
        )
        AUX[pl.ds(4 + 2 * ex, 2), :] = jnp.dot(
            grp[ex].astype(F32), spr[...], preferred_element_type=F32,
            precision=lax.Precision.HIGHEST,
        )
    for ex in range(2):
        for ey in range(2):
            row = AUX[pl.ds(2 * ex + ey, 1), :]
            KAP[pl.ds(16 * ex + 8 * ey, 8), :] = jnp.broadcast_to(row, (8, 128))

    half = jnp.float32(0.5)
    imx = [one] * 16
    imx[0] = jnp.where(gx > 0, half, one)
    imx[7] = imx[8] = half
    imx[15] = jnp.where(gx < nx - 1, half, one)
    imz = one - half * (j7 + j0)
    imy0 = one - half * s7 - (half * has_b) * s0
    imy1 = one - half * s0 - (half * has_t) * s7
    imyz = jnp.concatenate([imy0 * imz, imy1 * imz], 0)
    for x in range(16):
        W[rows(x), :] = jnp.float32(WTS[x % 8]) * cp[0]
        IM[rows(x), :] = imx[x] * imyz

    load_f.wait()
    for c in range(4):
        for x in range(16):
            L4[rows(x, 256 * c), :] = zjoin(F[rows(x, 256 * c), :])
        xyjoin(L4, 256 * c)
    pl.semaphore_wait(barrier, len(mates))
    now = faces(L4, 4, 0, *set4, 0)
    pending += now
    side = []
    for d, (dx, dy) in enumerate(DIRS):
        copy = pltpu.make_async_remote_copy(
            AUX, AUXR.at[d], as_sem.at[d], ar_sem.at[d],
            device_id=nbr(dx, dy), device_id_type=MESH,
        )
        copy.start()
        side.append(copy)
    load_c.wait()
    rowsc = []
    for d, (dx, dy) in enumerate(DIRS):
        copy = pltpu.make_async_remote_copy(
            CX.at[8], CX.at[d], cs_sem.at[d], cr_sem.at[d],
            device_id=nbr(dx, dy), device_id_type=MESH,
        )
        copy.start()
        rowsc.append(copy)
    load_v.wait()
    V[...] = V[...] * W[...]
    finish(now, L4, 4, 0, rx4, ry4, rc4)
    for c in range(4):
        at = pl.ds(256 * c, 256)
        F[at, :] = L4[at, :] * IM[...]

    def channel(c, carry):
        base = pl.multiple_of(c * 256, 256)
        coef = jnp.where(c == 3, jnp.float32(1.0 / prandtl), one)
        T3[...] = zop(F[pl.ds(base, 256), :], 0)
        for ex in range(2):
            planes = [F[pl.ds(base + 16 * (8 * ex + a), 16), :] for a in range(8)]
            for i in range(8):
                x = 8 * ex + i
                gxp = xop(planes, DER[i])
                gyp = yop(planes[i], 0)
                gzp = T3[rows(x), :]
                adv = (
                    F[rows(x), :] * gxp + F[rows(x, 256), :] * gyp + F[rows(x, 512), :] * gzp
                )
                nuw = coef * V[rows(x), :]
                T1[rows(x), :] = nuw * gxp
                T2[rows(x), :] = yop(nuw * gyp, 1) + W[rows(x), :] * adv
                T3[rows(x), :] = nuw * gzp
        T3[...] = zop(T3[...], 1) + T2[...]
        for ex in range(2):
            planes = [T1[rows(8 * ex + a), :] for a in range(8)]
            for i in range(8):
                x = 8 * ex + i
                total = xop(planes, DER[:, i]) + T3[rows(x), :]
                L4[pl.ds(base + 16 * x, 16), :] = zjoin(-total)
        xyjoin(L4, base)
        return carry

    lax.fori_loop(0, 4, channel, 0)
    now = faces(L4, 4, 1, *set4, 1)
    pending += now

    for copy in side:
        copy.wait_recv()

    def where_from(ex, ey):
        dx = -1 if ex == 0 else (1 if ex == 3 else 0)
        dy = -1 if ey == 0 else (1 if ey == 3 else 0)
        lx = {0: 1, 1: 0, 2: 1, 3: 0}[ex]
        ly = {0: 1, 1: 0, 2: 1, 3: 0}[ey]
        return dx, dy, 2 * lx + ly

    def slot_of(dx, dy):
        return 8 if (dx, dy) == (0, 0) else DIRS.index((-dx, -dy))

    kgrid = []
    for ex in range(4):
        line = []
        for ey in range(4):
            dx, dy, local = where_from(ex, ey)
            slot = slot_of(dx, dy)
            valid = vx[dx] * vy[dy]
            if slot == 8:
                krow = AUX[pl.ds(local, 1), :]
                grow = AUX[pl.ds(4 + local, 1), :]
            else:
                krow = AUXR[slot, pl.ds(local, 1), :]
                grow = AUXR[slot, pl.ds(4 + local, 1), :]
            line.append(krow * valid)
            hit = jnp.abs(jnp.broadcast_to(grow, (4, 128)) - sub[0:4].astype(F32)) < half
            OH[4 * ex + ey] = jnp.where(hit, valid, zero)
        kgrid.append(line)

    xsets = [(0, 1), (1,), (1, 2), (2,), (2, 3)]
    xclass = [0] + [1] * 6 + [2, 2] + [3] * 6 + [4]

    def spread(grid):
        planes = []
        for members in xsets:
            e = []
            for ey in range(4):
                total = grid[members[0]][ey]
                for ex in members[1:]:
                    total = total + grid[ex][ey]
                e.append(jnp.broadcast_to(total, (8, 128)))
            low = e[1] + s0 * e[0] + s7 * e[2]
            high = e[2] + s0 * e[1] + s7 * e[3]
            planes.append(zjoin(jnp.concatenate([low, high], 0)))
        return planes

    kplanes = spread(kgrid)
    mult = one / imyz
    for x in range(16):
        wa = jnp.float32(WTS[x % 8])
        ka = jnp.float32(KLN[x % 8])
        diag = (ka * cp[0] + wa * cp[3]) * kplanes[xclass[x]] + (
            jnp.float32(sigma_p) * wa / imx[x]
        ) * cp[0] * mult
        INVD[rows(x), :] = one / diag

    group = lane // 32

    def ag_start(a, row):
        ag1[a, 0] = row
        out = []
        for k in range(1, ny):
            copy = pltpu.make_async_remote_copy(
                ag1.at[a, 0], ag1.at[a, k], gs_sem.at[a, 0, k], gr_sem.at[a, 0, k],
                device_id=y_mate(k), device_id_type=MESH,
            )
            copy.start()
            out.append(copy)
        return out

    def ag_second(a, copies):
        for copy in copies:
            copy.wait_recv()
        row = ag1[a, 0]
        for k in range(1, ny):
            row = row + ag1[a, k]
        wide = jnp.broadcast_to(row, (8, 128))
        message = jnp.zeros((8, 128), F32)
        for s in range(4):
            turned = wide if s == 0 else pltpu.roll(wide, 32 * s, 1)
            for g in range(4):
                to = (g + s) % 4
                if g == 3:
                    row_at, to_at = 2, 1
                else:
                    t = xc + (g - 1)
                    low = t < 0
                    high = t > XC - 1
                    row_at = jnp.where(low | high, 2, t // 4)
                    to_at = jnp.where(low, 3, jnp.where(high, 0, t % 4))
                take = (sub == row_at) & (group == to_at) & (group == to)
                message = message + jnp.where(take, turned, zero)
        ag2[a, 0] = message[0:4]
        out = []
        for k in range(1, nxc):
            copy = pltpu.make_async_remote_copy(
                ag2.at[a, 0], ag2.at[a, k], gs_sem.at[a, 1, k], gr_sem.at[a, 1, k],
                device_id=x_mate(k), device_id_type=MESH,
            )
            copy.start()
            out.append(copy)
        return out

    def ag_third(a, copies):
        for copy in copies:
            copy.wait_recv()
        message = ag2[a, 0]
        for k in range(1, nxc):
            message = message + ag2[a, k]
        ag3[a, zc] = message
        out = []
        for k in range(1, nz):
            copy = pltpu.make_async_remote_copy(
                ag3.at[a, zc], ag3.at[a, zc], gs_sem.at[a, 2, k], gr_sem.at[a, 2, k],
                device_id=z_mate(k), device_id_type=MESH,
            )
            copy.start()
            out.append(copy)
        return out

    def ag_end(a, copies):
        for copy in copies:
            copy.wait_recv()

    def sums(a, count):
        total = ag3[a, 0][2:3]
        for z in range(1, nz):
            total = total + ag3[a, z][2:3]
        lanes = lane[0:1]
        return [
            jnp.sum(jnp.where(lanes == 32 + k, total, zero), axis=1, keepdims=True)
            for k in range(count)
        ]

    devs = [(dx, dy) for dx in (-1, 0, 1) for dy in (-1, 0, 1)]
    members = {dev: [] for dev in devs}
    for ex in range(4):
        for ey in range(4):
            dx, dy, _ = where_from(ex, ey)
            members[(dx, dy)].append((ex, ey))

    def restricted(L):
        x_first = imx[0] * L[rows(0), :]
        x_last = imx[15] * L[rows(15), :]
        low, high = x_first, x_last
        for x in range(1, 7):
            low = low + L[rows(x), :]
            high = high + L[rows(x + 8), :]
        low = low + half * L[rows(7), :]
        high = high + half * L[rows(8), :]
        grid = []
        for part in (x_first, low, high, x_last):
            part = part * imyz
            t0, t1 = part[0:8], part[8:16]
            grid.append(
                [
                    t0[0:1],
                    jnp.sum(t0, axis=0, keepdims=True),
                    jnp.sum(t1, axis=0, keepdims=True),
                    t1[7:8],
                ]
            )
        message = jnp.zeros((4, 128), F32)
        for dx, dy in devs:
            acc = None
            for ex, ey in members[(dx, dy)]:
                term = jnp.broadcast_to(grid[ex][ey], (4, 128)) * OH[4 * ex + ey]
                acc = term if acc is None else acc + term
            value = jnp.sum(acc, axis=1, keepdims=True)
            to = 32 * (dx + 1) + ((gy + dy + YL) % YL) * NCD + sub[0:4]
            message = message + jnp.where(lane[0:4] == to, value, zero)
        return jnp.sum(message, axis=0, keepdims=True)

    def with_sums(row, values):
        lanes = lane[0:1]
        for k, value in enumerate(values):
            row = row + jnp.where(lanes == 96 + k, value, zero)
        return row

    def coarse_planes(a):
        lanes = lane[0:1]
        accs = [None] * 9
        for z in range(nz):
            own = ag3[a, z]
            first, second = own[0:1], own[1:2]
            if z > 0:
                first = first + jnp.where(lanes < 32, ag3[a, z - 1][2:3], zero)
            if z < nz - 1:
                second = second + jnp.where(lanes >= 96, ag3[a, z + 1][2:3], zero)
            for h, part in enumerate((first, second)):
                wide = jnp.broadcast_to(part, (4, 128))
                for n in range(9):
                    term = CX[n, :, pl.ds((2 * z + h) * 128, 128)] * wide
                    accs[n] = term if accs[n] is None else accs[n] + term
        values = [jnp.sum(acc, axis=1, keepdims=True) for acc in accs]
        grid = []
        for ex in range(4):
            line = []
            for ey in range(4):
                dx, dy, _ = where_from(ex, ey)
                value = values[slot_of(dx, dy)]
                line.append(jnp.sum(OH[4 * ex + ey] * value, axis=0, keepdims=True))
            grid.append(line)
        return [plane * imyz for plane in spread(grid)]

    def apply_local(q, put):
        T3[...] = zop(q[...], 2)
        for ex in range(2):
            planes = [q[rows(8 * ex + a), :] for a in range(8)]
            kap = KAP[pl.ds(16 * ex, 16), :]
            for i in range(8):
                x = 8 * ex + i
                wa = jnp.float32(WTS[i])
                kx = xop(planes, STF[i])
                ky = yop(planes[i], 2)
                inner = cp[0] * kx + wa * (cp[1] * ky + cp[2] * T3[rows(x), :])
                put(x, planes[i], kap * inner + (jnp.float32(sigma_p) * wa) * (cp[0] * planes[i]))

    def put_joined(x, plane, value):
        L1[rows(x), :] = zjoin(value)

    upper = SBOUND
    lower = cheb_ratio * upper
    theta = 0.5 * (upper + lower)
    delta = 0.5 * (upper - lower)
    rho = delta / theta
    rho_next = 1.0 / (2.0 * theta / delta - rho)
    c2 = 2.0 * rho_next / delta
    c1 = jnp.float32((1.0 + rho_next * rho) / theta + c2)
    c2 = jnp.float32(c2 / theta)

    finish(now, L4, 4, 1, rx4, ry4, rc4)
    for x in range(16):
        scale = (jnp.float32(dt_step / WTS[x % 8]) * imx[x]) * (imyz * cp[4])
        for c in range(4):
            at = rows(x, 256 * c)
            FN[at, :] = F[at, :] + L4[at, :] * scale
    store_f = pltpu.make_async_copy(FN, out_f, l_sem.at[3])
    store_f.start()
    T3[...] = zop(FN[pl.ds(512, 256), :], 0)
    for ex in range(2):
        planes = [FN[rows(8 * ex + a), :] for a in range(8)]
        for i in range(8):
            x = 8 * ex + i
            div = xop(planes, DER[i]) + yop(FN[rows(x, 256), :], 0) + T3[rows(x), :]
            L1[rows(x), :] = zjoin(-(W[rows(x), :] * div))
    xyjoin(L1)

    ga = ag_start(0, restricted(L1))
    now = faces(L1, 1, 0, *set1, 2)
    pending += now
    pend_g = list(ga)
    finish(now, L1, 1, 0, rx1, ry1, rc1)
    R0[...] = L1[...]
    T1[...] = L1[...] * INVD[...]
    apply_local(T1, put_joined)
    xyjoin(L1)
    now = faces(L1, 1, 1, *set1, 3)
    pending += now
    ga = ag_second(0, ga)
    pend_g += ga
    ga = ag_third(0, ga)
    pend_g += ga
    finish(now, L1, 1, 1, rx1, ry1, rc1)
    S0[...] = c1 * T1[...] - c2 * (INVD[...] * L1[...])
    for copy in rowsc:
        copy.wait_recv()
    ag_end(0, ga)
    planes = coarse_planes(0)
    for x in range(16):
        Z0[rows(x), :] = S0[rows(x), :] + imx[x] * planes[xclass[x]]

    dot = []

    def put_first(x, plane, value):
        W1[rows(x), :] = value
        L1[rows(x), :] = zjoin(value)
        term = plane * value
        dot.append(term if not dot else dot.pop() + term)

    def full(v):
        return jnp.sum(jnp.sum(v, axis=0, keepdims=True), axis=1, keepdims=True)

    apply_local(Z0, put_first)
    xyjoin(L1)
    rz_part = None
    for x in range(16):
        term = imx[x] * (R0[rows(x), :] * Z0[rows(x), :])
        rz_part = term if rz_part is None else rz_part + term
    row = with_sums(restricted(L1), [full(rz_part * imyz), full(dot.pop())])
    ga = ag_start(1, row)
    pend_g += ga
    now = faces(L1, 1, 2, *set1, 4)
    pending += now
    finish(now, L1, 1, 2, rx1, ry1, rc1)
    T2[...] = L1[...]
    T1[...] = L1[...] * INVD[...]
    apply_local(T1, put_joined)
    xyjoin(L1)
    now = faces(L1, 1, 3, *set1, 5)
    pending += now
    ga = ag_second(1, ga)
    pend_g += ga
    ga = ag_third(1, ga)
    pend_g += ga
    finish(now, L1, 1, 3, rx1, ry1, rc1)
    ZI[...] = c1 * T1[...] - c2 * (INVD[...] * L1[...])
    ag_end(1, ga)
    rz0, curv0 = sums(1, 2)
    step0 = rz0 / curv0
    planes = coarse_planes(1)
    rz_part = None
    for x in range(16):
        at = rows(x)
        zi = ZI[at, :] + imx[x] * planes[xclass[x]]
        z1 = Z0[at, :] - step0 * zi
        ZI[at, :] = z1
        term = imx[x] * ((R0[at, :] - step0 * T2[at, :]) * z1)
        rz_part = term if rz_part is None else rz_part + term

    dots = [None, None]

    def put_second(x, plane, value):
        terms = (plane * value, Z0[rows(x), :] * value + plane * W1[rows(x), :])
        for k in range(2):
            dots[k] = terms[k] if dots[k] is None else dots[k] + terms[k]

    apply_local(ZI, put_second)
    row = with_sums(
        jnp.zeros((1, 128), F32), [full(rz_part * imyz), full(dots[0]), full(dots[1])]
    )
    ga = ag_start(2, row)
    pend_g += ga
    ga = ag_second(2, ga)
    pend_g += ga
    ga = ag_third(2, ga)
    pend_g += ga
    ag_end(2, ga)
    rz1, a11, a10 = sums(2, 3)
    beta = rz1 / rz0
    curv1 = a11 + beta * a10 + beta * beta * curv0
    step1 = rz1 / curv1
    PC[...] = (step0 + step1 * beta) * Z0[...] + step1 * ZI[...]
    store_p = pltpu.make_async_copy(PC, out_p, l_sem.at[4])
    store_p.start()

    for copy in pending + side + rowsc + pend_g:
        copy.wait_send()
    store_f.wait()
    store_p.wait()


def per_device(nx, ny, nxc, fields, viscosity, inv_density, elem_group, coarse_inverse):
    nz = nx // nxc
    cy, bz, cp, spr = constants()
    coarse = coarse_inverse
    if nxc * ny != XC * YL:
        coarse = coarse.reshape(NCD, nz, nxc, ny, NCD)
        coarse = jnp.pad(coarse, ((0, 0), (0, 0), (0, XC - nxc), (0, YL - ny), (0, 0)))
        coarse = coarse.reshape(NCD, nz * XC * YL * NCD)
    ncp = coarse.shape[1]

    def vm(*shape):
        return pltpu.VMEM(shape, F32)

    field = vm(256, 128)
    scratch = [
        vm(1024, 128), vm(1024, 128), field, vm(1024, 128), field, field, field,
        vm(32, 128), field, vm(9, NCD, ncp), vm(8, 128), vm(8, 8, 128), vm(16, 4, 128), field,
        field, field, field, field, field, field, field, field,
        vm(2, 2, 64, 128), vm(2, 2, 64, 128), vm(2, 4, 4, 128),
        vm(2, 2, 64, 128), vm(2, 2, 64, 128), vm(2, 4, 4, 128),
        vm(4, 2, 16, 128), vm(4, 2, 16, 128), vm(4, 4, 1, 128),
        vm(4, 2, 16, 128), vm(4, 2, 16, 128), vm(4, 4, 1, 128),
        vm(3, ny, 1, 128), vm(3, nxc, 4, 128), vm(3, nz, 4, 128),
        pltpu.SemaphoreType.DMA((6, 8)), pltpu.SemaphoreType.DMA((6, 8)),
        pltpu.SemaphoreType.DMA((8,)), pltpu.SemaphoreType.DMA((8,)),
        pltpu.SemaphoreType.DMA((8,)), pltpu.SemaphoreType.DMA((8,)),
        pltpu.SemaphoreType.DMA((3, 3, 12)), pltpu.SemaphoreType.DMA((3, 3, 12)),
        pltpu.SemaphoreType.DMA((5,)),
    ]
    anywhere = pl.BlockSpec(memory_space=pl.ANY)
    inside = pl.BlockSpec(memory_space=pltpu.VMEM)
    new, pressure = pl.pallas_call(
        functools.partial(kernel, nx, ny, nxc),
        out_shape=(
            jax.ShapeDtypeStruct((1024, 128), F32),
            jax.ShapeDtypeStruct((256, 128), F32),
        ),
        in_specs=[anywhere, anywhere, inside, inside, anywhere, inside, inside, inside, inside],
        out_specs=(anywhere, anywhere),
        scratch_shapes=scratch,
        compiler_params=pltpu.CompilerParams(collective_id=0, has_side_effects=True),
    )(
        fields.reshape(1024, 128),
        viscosity.reshape(256, 128),
        inv_density,
        elem_group,
        coarse,
        cy, bz, cp, spr,
    )
    return new.reshape(fields.shape), pressure.reshape(viscosity.shape)


def build(mesh, nxc):
    placed = (
        P(None, "gx", None, "gy", None, None),
        P("gx", None, "gy", None, None),
        P("gx", "gy", None),
        P("gx", "gy", None),
        P(("gx", "gy"), None),
    )
    return jax.shard_map(
        functools.partial(per_device, mesh.shape["gx"], mesh.shape["gy"], nxc),
        mesh=mesh,
        in_specs=placed,
        out_specs=(P(None, "gx", None, "gy", None, None), P("gx", None, "gy", None, None)),
        check_vma=False,
    )


def solution(mesh):
    return build(mesh, XC)
```

time: 732 us -> 83.3 us (0.11)
  blocking collectives: 562 us -> 0 us
  Pallas kernels: 0 us -> 79.9 us
  starting transfers between devices: 72.1 us -> 0 us
  waiting for transfers between devices: 45.5 us -> 0 us
  matrix products: 18.4 us -> 0 us
  local copies, waits for them, and re-layouts: 14 us -> 2.56 us
    psum x3 -> x0, blocking collectives: 334 us -> none  [total(): return lax.psum(value, ('gx', 'gy'))]
    unnamed x2 -> x0, blocking collectives: 228 us -> none
    pallas_call x0 -> x1, Pallas kernels: none -> 79.9 us  [per_device(): pl.pallas_call(functools.partial(kernel, nx, ny, nxc), out_shape=(jax.Sha...]
    ppermute x28 -> x0, starting transfers between devices: 72.1 us -> none  [the longest x14 40.6 us: with_halo(): lax.ppermute(tail, axis, [(i, (i + 1) % count) for i in range(ends)])]
    ppermute x28 -> x0, waiting for transfers between devices: 45.5 us -> none  [the longest x14 45.5 us: with_halo(): lax.ppermute(head, axis, [((i + 1) % count, i) for i in range(ends)])]
    dot_general x51 -> x0, matrix products: 18.4 us -> none  [the longest x7 4.23 us: assemble(): return jnp.matmul(field, pair_table, precision=precision)]
  transfers between devices with their start and end apart: 28 -> 0, of which waited for: 14 -> 0; matrix products, arithmetic and copies ran while one was open for 0% -> 0% of each run, Pallas kernels for 0% -> 0%
where the time goes in v1:
time: 83.3 us; the launch traced here: 83.1 us
  Pallas kernels  79.9 us (96%)
  local copies, waits for them, and re-layouts  2.56 us (3%)
    pallas_call x1, Pallas kernels, per_device(): pl.pallas_call(functools.partial(kernel, nx, ny, nxc), out_shape=(jax.Sha...  79.9 us
    unnamed x4, local copies, waits for them, and re-layouts  2.56 us

profile of v1, /device:TPU:1, one launch (start us, length us, event | category | flops | bytes accessed | tf_op | source)
XLA Modules:
  0.0 83.1 jit_solution(14735871223342265401)
XLA Ops:
  0.6 79.9 %shard_map.104 = (f32[1024,128]{1,0:T(8,128)}, f32[256,128]{1,0:T(8,128)}) custom-call(f32[1024,128]{1,0:T(8,128)} %bitcast.4, f32[256,128]{1,0:T(8,128)} %bitcast.6, f32[2,2,16]{2,1,0:T(2,128)} %dens.1, s32[2,2,16]{2,1,0:T(2,128)} %grp.1, f32[4,3072]{1,0:T(4,128)} %coarse.1, f32[3,8,8,128]{3,2,1,0:T(8,128)} %constant.8.clone.cy, ...), custom_call_target="tpu_custom_call" | custom-call | tf_op jit(solution)/shard_map/pallas_call | solution.py:719
  80.5 0.0 copy-start
  80.5 1.9 %copy.13 = f32[4,2,8,2,8,128]{5,4,3,2,1,0:T(8,128)} copy(f32[4,2,8,2,8,128]{5,4,3,2,1,0:T(8,128)} %bitcast.5) | data formatting | bytes 1048576
  82.5 0.0 copy-done
  82.5 0.7 copy.14
Async XLA Ops:
  80.5 1.9 %copy-start = (f32[256,128]{1,0:T(8,128)S(1)}, f32[256,128]{1,0:T(8,128)}, u32[]{:S(2)}) copy-start(f32[256,128]{1,0:T(8,128)} %get-tuple-element.5) | copy-start | bytes 393220

commit v2 on v1

--- a/solution.py
+++ b/solution.py
@@ -69,17 +69,70 @@
 KLN = np.diag(STF)
 
 
+def functionals():
+    count = 8
+    found = []
+    for first in (3, 0, count - 2):
+        both = np.zeros((2, 6, 16))
+        mult = np.ones((count, 8))
+        mult[1:, 0] = 2.0
+        mult[:-1, 7] = 2.0
+        for place in range(6):
+            e = first - 2 + place
+            if not 0 <= e < count:
+                continue
+            phi = np.zeros((count, 8))
+            phi[e] = 1.0 / mult[e]
+            if e > 0:
+                phi[e - 1, 7] = phi[e, 0]
+            if e < count - 1:
+                phi[e + 1, 0] = phi[e, 7]
+            t = -(phi * WTS[None, :]) @ DER
+            joint = t[:-1, 7] + t[1:, 0]
+            t[:-1, 7] = joint
+            t[1:, 0] = joint
+            t = t / (mult * WTS[None, :])
+            both[0, place] = t[first : first + 2].reshape(16)
+            both[1, place] = phi[first : first + 2].reshape(16)
+        found.append(both)
+    return np.stack(found, 0)
+
+
+def z_functional():
+    mult = np.ones((16, 8))
+    mult[1:, 0] = 2.0
+    mult[:-1, 7] = 2.0
+    full = np.zeros((128, 128))
+    for e in range(16):
+        phi = np.zeros((16, 8))
+        phi[e] = 1.0 / mult[e]
+        if e > 0:
+            phi[e - 1, 7] = phi[e, 0]
+        if e < 15:
+            phi[e + 1, 0] = phi[e, 7]
+        t = -(phi * WTS[None, :]) @ DER
+        joint = t[:-1, 7] + t[1:, 0]
+        t[:-1, 7] = joint
+        t[1:, 0] = joint
+        t = t / (mult * WTS[None, :])
+        full[:, 8 * e : 8 * e + 8] = t.reshape(128)[:, None] / 8.0
+    return full
+
+
+FUN = functionals()
+
+
 def constants():
     cols = np.stack([DER, DER.T, STF], 0)
     cy = np.broadcast_to(np.transpose(cols, (0, 2, 1))[:, :, :, None], (3, 8, 8, 128))
 
     def big(one):
-        full = np.kron(np.eye(16), one).astype(np.float32)
+        full = (one if one.shape[0] == 128 else np.kron(np.eye(16), one)).astype(np.float32)
         high = np.asarray(full, dtype=jnp.bfloat16)
         low = np.asarray(full - high.astype(np.float32), dtype=jnp.bfloat16)
         return np.block([[high, low], [high, np.zeros_like(low)]])
 
-    bz = np.stack([big(DER.T), big(DER), big(STF)], 0)
+    bz = np.stack([big(DER.T), big(DER), big(STF), big(z_functional())], 0)
     wy = np.tile(WTS, 2)[:, None]
     ky = np.tile(KLN, 2)[:, None]
     wz = np.tile(WTS, 16)[None, :]
@@ -87,22 +140,26 @@
     one = np.ones((16, 128))
     cp = np.stack([wy * wz, one * wz, wy * one, ky * wz + wy * kz, 1.0 / (wy * wz)], 0)
     spread = np.kron(np.eye(16), np.ones((1, 8)))
+    fy = np.stack([FUN[0], FUN[1] - FUN[0], FUN[2] - FUN[0]], 0).reshape(36, 16)
+    fy = np.broadcast_to(fy[:, :, None], (36, 16, 128))
     return (
         jnp.asarray(np.ascontiguousarray(cy), F32),
         jnp.asarray(bz, BF16),
         jnp.asarray(cp, F32),
         jnp.asarray(spread, F32),
+        jnp.asarray(np.ascontiguousarray(fy), F32),
     )
 
 
 def kernel(
     nx, ny, nxc,
-    fields, visc, dens, grp, coarse, cy, bz, cp, spr,
+    fields, visc, dens_h, grp_h, coarse, cy_h, bz_h, cp_h, spr_h, fy_h,
     out_f, out_p,
+    dens, grp, cy, bz, cp, spr, fy, YF, G, TR,
     F, FN, V, L4, L1, W, IM, KAP, INVD, CX, AUX, AUXR, OH, PC,
     T1, T2, T3, R0, S0, Z0, W1, ZI,
     sx4, sy4, sc4, rx4, ry4, rc4, sx1, sy1, sc1, rx1, ry1, rc1,
-    ag1, ag2, ag3,
+    ag1, ag3,
     s_sem, r_sem, as_sem, ar_sem, cs_sem, cr_sem, gs_sem, gr_sem, l_sem,
 ):
     gx = lax.axis_index("gx")
@@ -114,29 +171,45 @@
     def nbr(dx, dy):
         return ((gx + dx + nx) % nx, (gy + dy + ny) % ny)
 
-    def y_mate(k):
-        return (gx, (gy + k) % ny)
-
-    def x_mate(k):
-        return (zc * nxc + (xc + k) % nxc, gy)
-
     def z_mate(k):
         return (((zc + k) % nz) * nxc + xc, gy)
 
-    mates = [nbr(dx, dy) for dx, dy in DIRS]
-    mates += [y_mate(k) for k in range(1, ny)]
-    mates += [x_mate(k) for k in range(1, nxc)]
-    mates += [z_mate(k) for k in range(1, nz)]
+    def hops(off):
+        dx, dy = off
+        chips = dx // 2
+        return min(chips, nxc // 2 - chips) + min(dy, ny - dy)
+
+    flat = [(dx, dy) for dx in range(nxc) for dy in range(ny)][1:]
+    flat.sort(key=hops, reverse=True)
+    zline = sorted(range(1, nz), key=lambda k: -min(k, nz - k))
+
+    def p_mate(dx, dy):
+        return (zc * nxc + (xc + dx) % nxc, (gy + dy) % ny)
+
+    mates = [nbr(dx, dy) for dx, dy in DIRS if dx != 0]
+    mates += [p_mate(*off) for off in flat]
+    mates += [z_mate(k) for k in zline]
+    if nxc * ny < 4:
+        mates += [nbr(0, -1), nbr(0, 1)]
     barrier = pltpu.get_barrier_semaphore()
     for mate in mates:
         pl.semaphore_signal(barrier, inc=1, device_id=mate, device_id_type=MESH)
 
-    load_f = pltpu.make_async_copy(fields, F, l_sem.at[0])
-    load_v = pltpu.make_async_copy(visc, V, l_sem.at[1])
-    load_c = pltpu.make_async_copy(coarse, CX.at[8], l_sem.at[2])
-    load_f.start()
-    load_v.start()
-    load_c.start()
+    load_f = []
+    for c in range(4):
+        part = pl.ds(256 * c, 256)
+        load_f.append(pltpu.make_async_copy(fields.at[part], F.at[part], l_sem.at[c]))
+    small = [(dens_h, dens), (grp_h, grp), (spr_h, spr), (cp_h, cp)]
+    large = [(cy_h, cy), (bz_h, bz), (visc, V), (fy_h, fy)]
+    load_s = [
+        pltpu.make_async_copy(src, dst, l_sem.at[4 + k]) for k, (src, dst) in enumerate(small)
+    ]
+    load_l = [
+        pltpu.make_async_copy(src, dst, l_sem.at[8 + k]) for k, (src, dst) in enumerate(large)
+    ]
+    load_c = pltpu.make_async_copy(coarse, CX.at[8], l_sem.at[12])
+    for copy in load_f + load_s + load_l + [load_c]:
+        copy.start()
 
     lane = lax.broadcasted_iota(jnp.int32, (8, 128), 1)
     sub = lax.broadcasted_iota(jnp.int32, (8, 128), 0)
@@ -241,6 +314,16 @@
     set1 = (sx1, sy1, sc1, rx1, ry1, rc1)
     pending = []
 
+    for c in range(4):
+        load_f[c].wait()
+        for x in range(16):
+            L4[rows(x, 256 * c), :] = zjoin(F[rows(x, 256 * c), :])
+        xyjoin(L4, 256 * c)
+    pl.semaphore_wait(barrier, len(mates))
+    now = faces(L4, 4, 0, *set4, 0)
+    pending += now
+    for copy in load_s:
+        copy.wait()
     for ex in range(2):
         AUX[pl.ds(2 * ex, 2), :] = jnp.dot(
             dens[ex], spr[...], preferred_element_type=F32, precision=lax.Precision.HIGHEST
@@ -254,6 +337,23 @@
             row = AUX[pl.ds(2 * ex + ey, 1), :]
             KAP[pl.ds(16 * ex + 8 * ey, 8), :] = jnp.broadcast_to(row, (8, 128))
 
+    side = []
+    for d, (dx, dy) in enumerate(DIRS):
+        copy = pltpu.make_async_remote_copy(
+            AUX, AUXR.at[d], as_sem.at[d], ar_sem.at[d],
+            device_id=nbr(dx, dy), device_id_type=MESH,
+        )
+        copy.start()
+        side.append(copy)
+    rowsc = []
+    for d, (dx, dy) in enumerate(DIRS):
+        copy = pltpu.make_async_remote_copy(
+            coarse, CX.at[d], cs_sem.at[d], cr_sem.at[d],
+            device_id=nbr(dx, dy), device_id_type=MESH,
+        )
+        copy.start()
+        rowsc.append(copy)
+
     half = jnp.float32(0.5)
     imx = [one] * 16
     imx[0] = jnp.where(gx > 0, half, one)
@@ -267,37 +367,44 @@
         W[rows(x), :] = jnp.float32(WTS[x % 8]) * cp[0]
         IM[rows(x), :] = imx[x] * imyz
 
-    load_f.wait()
-    for c in range(4):
-        for x in range(16):
-            L4[rows(x, 256 * c), :] = zjoin(F[rows(x, 256 * c), :])
-        xyjoin(L4, 256 * c)
-    pl.semaphore_wait(barrier, len(mates))
-    now = faces(L4, 4, 0, *set4, 0)
-    pending += now
-    side = []
-    for d, (dx, dy) in enumerate(DIRS):
-        copy = pltpu.make_async_remote_copy(
-            AUX, AUXR.at[d], as_sem.at[d], ar_sem.at[d],
-            device_id=nbr(dx, dy), device_id_type=MESH,
-        )
-        copy.start()
-        side.append(copy)
-    load_c.wait()
-    rowsc = []
-    for d, (dx, dy) in enumerate(DIRS):
-        copy = pltpu.make_async_remote_copy(
-            CX.at[8], CX.at[d], cs_sem.at[d], cr_sem.at[d],
-            device_id=nbr(dx, dy), device_id_type=MESH,
-        )
-        copy.start()
-        rowsc.append(copy)
-    load_v.wait()
+    for copy in load_l + [load_c]:
+        copy.wait()
     V[...] = V[...] * W[...]
+    no_b, no_t = one - has_b, one - has_t
+    for k in range(12):
+        YF[k] = fy[k] + no_b * fy[12 + k] + no_t * fy[24 + k]
     finish(now, L4, 4, 0, rx4, ry4, rc4)
     for c in range(4):
         at = pl.ds(256 * c, 256)
         F[at, :] = L4[at, :] * IM[...]
+
+    for copy in side:
+        copy.wait_recv()
+
+    def where_from(ex, ey):
+        return ex // 2 - 1, ey // 2 - 1, 2 * (ex % 2) + ey % 2
+
+    def slot_of(dx, dy):
+        return 8 if (dx, dy) == (0, 0) else DIRS.index((-dx, -dy))
+
+    around = [
+        (ex, ey) for ex in range(6) for ey in range(6) if not (ex in (0, 5) and ey in (0, 5))
+    ]
+    kgrid = [[None] * 4 for _ in range(4)]
+    for ex, ey in around:
+        dx, dy, local = where_from(ex, ey)
+        slot = slot_of(dx, dy)
+        valid = vx[dx] * vy[dy]
+        if slot == 8:
+            krow = AUX[pl.ds(local, 1), :]
+            grow = AUX[pl.ds(4 + local, 1), :]
+        else:
+            krow = AUXR[slot, pl.ds(local, 1), :]
+            grow = AUXR[slot, pl.ds(4 + local, 1), :]
+        if 1 <= ex <= 4 and 1 <= ey <= 4:
+            kgrid[ex - 1][ey - 1] = krow * valid
+        hit = jnp.abs(jnp.broadcast_to(grow, (4, 128)) - sub[0:4].astype(F32)) < half
+        OH[6 * ex + ey] = jnp.where(hit, valid, zero)
 
     def channel(c, carry):
         base = pl.multiple_of(c * 256, 256)
@@ -323,7 +430,9 @@
             for i in range(8):
                 x = 8 * ex + i
                 total = xop(planes, DER[:, i]) + T3[rows(x), :]
-                L4[pl.ds(base + 16 * x, 16), :] = zjoin(-total)
+                at = pl.ds(base + 16 * x, 16)
+                G[at, :] = W[rows(x), :] * F[at, :] - jnp.float32(dt_step) * total
+                L4[at, :] = zjoin(-total)
         xyjoin(L4, base)
         return carry
 
@@ -331,36 +440,175 @@
     now = faces(L4, 4, 1, *set4, 1)
     pending += now
 
-    for copy in side:
-        copy.wait_recv()
-
-    def where_from(ex, ey):
-        dx = -1 if ex == 0 else (1 if ex == 3 else 0)
-        dy = -1 if ey == 0 else (1 if ey == 3 else 0)
-        lx = {0: 1, 1: 0, 2: 1, 3: 0}[ex]
-        ly = {0: 1, 1: 0, 2: 1, 3: 0}[ey]
-        return dx, dy, 2 * lx + ly
-
-    def slot_of(dx, dy):
-        return 8 if (dx, dy) == (0, 0) else DIRS.index((-dx, -dy))
-
-    kgrid = []
-    for ex in range(4):
-        line = []
-        for ey in range(4):
-            dx, dy, local = where_from(ex, ey)
-            slot = slot_of(dx, dy)
-            valid = vx[dx] * vy[dy]
-            if slot == 8:
-                krow = AUX[pl.ds(local, 1), :]
-                grow = AUX[pl.ds(4 + local, 1), :]
-            else:
-                krow = AUXR[slot, pl.ds(local, 1), :]
-                grow = AUXR[slot, pl.ds(4 + local, 1), :]
-            line.append(krow * valid)
-            hit = jnp.abs(jnp.broadcast_to(grow, (4, 128)) - sub[0:4].astype(F32)) < half
-            OH[4 * ex + ey] = jnp.where(hit, valid, zero)
-        kgrid.append(line)
+    group = lane[0:1] // 32
+    parts = [jnp.where(group == g, one, zero) for g in range(4)]
+
+    def ag_start(a, row):
+        ag1[a, xc, 0] = row
+        out = []
+        for dx, dy in flat:
+            copy = pltpu.make_async_remote_copy(
+                ag1.at[a, xc, 0], ag1.at[a, xc, dy],
+                gs_sem.at[a, dx * ny + dy], gr_sem.at[a, dx * ny + dy],
+                device_id=p_mate(dx, dy), device_id_type=MESH,
+            )
+            copy.start()
+            out.append(copy)
+        return out
+
+    def ag_second(a, copies, only_sums=False):
+        for copy in copies:
+            copy.wait_recv()
+        pre = [[None] * 3 for _ in range(4)]
+        for xs in range(nxc):
+            row = ag1[a, xs, 0]
+            for k in range(1, ny):
+                row = row + ag1[a, xs, k]
+            for g in range(3, 4) if only_sums else range(4):
+                t = xs + g - 1
+                if g == 3:
+                    row_at, to_at = 2, 1
+                elif t < 0:
+                    row_at, to_at = 2, 3
+                elif t > nxc - 1:
+                    row_at, to_at = 2, 0
+                else:
+                    row_at, to_at = t // 4, t % 4
+                turn = (to_at - g) % 4
+                part = row * parts[g]
+                old = pre[turn][row_at]
+                pre[turn][row_at] = part if old is None else old + part
+        blank = jnp.zeros((1, 128), F32)
+        message = None
+        for turn in range(4):
+            if all(row is None for row in pre[turn]):
+                continue
+            block = [blank if row is None else row for row in pre[turn]] + [blank] * 5
+            block = jnp.concatenate(block, 0)
+            if turn:
+                block = pltpu.roll(block, 32 * turn, 1)
+            message = block if message is None else message + block
+        ag3[a, zc] = message[0:4]
+        out = []
+        for k in zline:
+            copy = pltpu.make_async_remote_copy(
+                ag3.at[a, zc], ag3.at[a, zc], gs_sem.at[a, 64 + k], gr_sem.at[a, 64 + k],
+                device_id=z_mate(k), device_id_type=MESH,
+            )
+            copy.start()
+            out.append(copy)
+        return out
+
+    def ag_end(a, copies):
+        for copy in copies:
+            copy.wait_recv()
+
+    def sums(a, count):
+        total = ag3[a, 0][2:3]
+        for z in range(1, nz):
+            total = total + ag3[a, z][2:3]
+        lanes = lane[0:1]
+        return [
+            jnp.sum(jnp.where(lanes == 32 + k, total, zero), axis=1, keepdims=True)
+            for k in range(count)
+        ]
+
+    devs = [(dx, dy) for dx in (-1, 0, 1) for dy in (-1, 0, 1)]
+    members = {dev: [] for dev in devs}
+    for ex, ey in around:
+        dx, dy, _ = where_from(ex, ey)
+        members[(dx, dy)].append((ex, ey))
+
+    def restricted(L):
+        x_first = imx[0] * L[rows(0), :]
+        x_last = imx[15] * L[rows(15), :]
+        low, high = x_first, x_last
+        for x in range(1, 7):
+            low = low + L[rows(x), :]
+            high = high + L[rows(x + 8), :]
+        low = low + half * L[rows(7), :]
+        high = high + half * L[rows(8), :]
+        grid = {}
+        for ex, part in enumerate((x_first, low, high, x_last)):
+            part = part * imyz
+            t0, t1 = part[0:8], part[8:16]
+            grid[ex + 1, 1] = t0[0:1]
+            grid[ex + 1, 2] = jnp.sum(t0, axis=0, keepdims=True)
+            grid[ex + 1, 3] = jnp.sum(t1, axis=0, keepdims=True)
+            grid[ex + 1, 4] = t1[7:8]
+        return share(grid)
+
+    def share(grid):
+        message = jnp.zeros((4, 128), F32)
+        for dx, dy in devs:
+            acc = None
+            for ex, ey in members[(dx, dy)]:
+                if (ex, ey) not in grid:
+                    continue
+                term = jnp.broadcast_to(grid[ex, ey], (4, 128)) * OH[6 * ex + ey]
+                acc = term if acc is None else acc + term
+            value = jnp.sum(acc, axis=1, keepdims=True)
+            to = 32 * (dx + 1) + ((gy + dy + YL) % YL) * NCD + sub[0:4]
+            message = message + jnp.where(lane[0:4] == to, value, zero)
+        return jnp.sum(message, axis=0, keepdims=True)
+
+    def along(table, ex, x):
+        c0 = FUN[0, table, ex, x]
+        cl, cr = FUN[1, table, ex, x] - c0, FUN[2, table, ex, x] - c0
+        if max(abs(c0), abs(cl), abs(cr)) < 1e-12:
+            return None
+        value = jnp.float32(c0)
+        if abs(cl) > 1e-12:
+            value = value + jnp.float32(cl) * (one - has_l)
+        if abs(cr) > 1e-12:
+            value = value + jnp.float32(cr) * (one - has_r)
+        return value
+
+    def restricted_early():
+        TR[...] = jnp.zeros((2, 40, 128), F32)
+        for ex in range(6):
+            summed = []
+            for c, table in ((0, 0), (1, 1), (2, 1)):
+                total = None
+                for x in range(16):
+                    coef = along(table, ex, x)
+                    if coef is None:
+                        continue
+                    term = coef * G[rows(x, 256 * c), :]
+                    total = term if total is None else total + term
+                summed.append(total)
+            for ey in range(6):
+                if (ex, ey) not in around:
+                    continue
+                at = pl.ds(6 * ex + ey, 1)
+                value = None
+                if 1 <= ey <= 4:
+                    value = YF[6 + ey] * summed[0]
+                if 1 <= ex <= 4:
+                    term = YF[ey] * summed[1]
+                    value = term if value is None else value + term
+                TR[0, at, :] = jnp.sum(value, axis=0, keepdims=True)
+                if 1 <= ex <= 4 and 1 <= ey <= 4:
+                    TR[1, at, :] = jnp.sum(YF[6 + ey] * summed[2], axis=0, keepdims=True)
+        last = zop(TR[1], 3)
+        grid = {}
+        for tile in range(5):
+            v = TR[0, pl.ds(8 * tile, 8), :] * imz
+            v = v + j7 * pltpu.roll(v, 127, 1) + j0 * pltpu.roll(v, 1, 1)
+            v = v + last[8 * tile : 8 * tile + 8]
+            for k in range(8):
+                if (8 * tile + k) // 6 < 6 and divmod(8 * tile + k, 6) in around:
+                    grid[divmod(8 * tile + k, 6)] = v[k : k + 1]
+        return share(grid)
+
+    def with_sums(row, values):
+        lanes = lane[0:1]
+        for k, value in enumerate(values):
+            row = row + jnp.where(lanes == 96 + k, value, zero)
+        return row
+
+    ga = ag_start(0, restricted_early())
+    pend_g = list(ga)
 
     xsets = [(0, 1), (1,), (1, 2), (2,), (2, 3)]
     xclass = [0] + [1] * 6 + [2, 2] + [3] * 6 + [4]
@@ -388,129 +636,6 @@
             jnp.float32(sigma_p) * wa / imx[x]
         ) * cp[0] * mult
         INVD[rows(x), :] = one / diag
-
-    group = lane // 32
-
-    def ag_start(a, row):
-        ag1[a, 0] = row
-        out = []
-        for k in range(1, ny):
-            copy = pltpu.make_async_remote_copy(
-                ag1.at[a, 0], ag1.at[a, k], gs_sem.at[a, 0, k], gr_sem.at[a, 0, k],
-                device_id=y_mate(k), device_id_type=MESH,
-            )
-            copy.start()
-            out.append(copy)
-        return out
-
-    def ag_second(a, copies):
-        for copy in copies:
-            copy.wait_recv()
-        row = ag1[a, 0]
-        for k in range(1, ny):
-            row = row + ag1[a, k]
-        wide = jnp.broadcast_to(row, (8, 128))
-        message = jnp.zeros((8, 128), F32)
-        for s in range(4):
-            turned = wide if s == 0 else pltpu.roll(wide, 32 * s, 1)
-            for g in range(4):
-                to = (g + s) % 4
-                if g == 3:
-                    row_at, to_at = 2, 1
-                else:
-                    t = xc + (g - 1)
-                    low = t < 0
-                    high = t > XC - 1
-                    row_at = jnp.where(low | high, 2, t // 4)
-                    to_at = jnp.where(low, 3, jnp.where(high, 0, t % 4))
-                take = (sub == row_at) & (group == to_at) & (group == to)
-                message = message + jnp.where(take, turned, zero)
-        ag2[a, 0] = message[0:4]
-        out = []
-        for k in range(1, nxc):
-            copy = pltpu.make_async_remote_copy(
-                ag2.at[a, 0], ag2.at[a, k], gs_sem.at[a, 1, k], gr_sem.at[a, 1, k],
-                device_id=x_mate(k), device_id_type=MESH,
-            )
-            copy.start()
-            out.append(copy)
-        return out
-
-    def ag_third(a, copies):
-        for copy in copies:
-            copy.wait_recv()
-        message = ag2[a, 0]
-        for k in range(1, nxc):
-            message = message + ag2[a, k]
-        ag3[a, zc] = message
-        out = []
-        for k in range(1, nz):
-            copy = pltpu.make_async_remote_copy(
-                ag3.at[a, zc], ag3.at[a, zc], gs_sem.at[a, 2, k], gr_sem.at[a, 2, k],
-                device_id=z_mate(k), device_id_type=MESH,
-            )
-            copy.start()
-            out.append(copy)
-        return out
-
-    def ag_end(a, copies):
-        for copy in copies:
-            copy.wait_recv()
-
-    def sums(a, count):
-        total = ag3[a, 0][2:3]
-        for z in range(1, nz):
-            total = total + ag3[a, z][2:3]
-        lanes = lane[0:1]
-        return [
-            jnp.sum(jnp.where(lanes == 32 + k, total, zero), axis=1, keepdims=True)
-            for k in range(count)
-        ]
-
-    devs = [(dx, dy) for dx in (-1, 0, 1) for dy in (-1, 0, 1)]
-    members = {dev: [] for dev in devs}
-    for ex in range(4):
-        for ey in range(4):
-            dx, dy, _ = where_from(ex, ey)
-            members[(dx, dy)].append((ex, ey))
-
-    def restricted(L):
-        x_first = imx[0] * L[rows(0), :]
-        x_last = imx[15] * L[rows(15), :]
-        low, high = x_first, x_last
-        for x in range(1, 7):
-            low = low + L[rows(x), :]
-            high = high + L[rows(x + 8), :]
-        low = low + half * L[rows(7), :]
-        high = high + half * L[rows(8), :]
-        grid = []
-        for part in (x_first, low, high, x_last):
-            part = part * imyz
-            t0, t1 = part[0:8], part[8:16]
-            grid.append(
-                [
-                    t0[0:1],
-                    jnp.sum(t0, axis=0, keepdims=True),
-                    jnp.sum(t1, axis=0, keepdims=True),
-                    t1[7:8],
-                ]
-            )
-        message = jnp.zeros((4, 128), F32)
-        for dx, dy in devs:
-            acc = None
-            for ex, ey in members[(dx, dy)]:
-                term = jnp.broadcast_to(grid[ex][ey], (4, 128)) * OH[4 * ex + ey]
-                acc = term if acc is None else acc + term
-            value = jnp.sum(acc, axis=1, keepdims=True)
-            to = 32 * (dx + 1) + ((gy + dy + YL) % YL) * NCD + sub[0:4]
-            message = message + jnp.where(lane[0:4] == to, value, zero)
-        return jnp.sum(message, axis=0, keepdims=True)
-
-    def with_sums(row, values):
-        lanes = lane[0:1]
-        for k, value in enumerate(values):
-            row = row + jnp.where(lanes == 96 + k, value, zero)
-        return row
 
     def coarse_planes(a):
         lanes = lane[0:1]
@@ -532,9 +657,9 @@
         for ex in range(4):
             line = []
             for ey in range(4):
-                dx, dy, _ = where_from(ex, ey)
+                dx, dy, _ = where_from(ex + 1, ey + 1)
                 value = values[slot_of(dx, dy)]
-                line.append(jnp.sum(OH[4 * ex + ey] * value, axis=0, keepdims=True))
+                line.append(jnp.sum(OH[6 * ex + ey + 7] * value, axis=0, keepdims=True))
             grid.append(line)
         return [plane * imyz for plane in spread(grid)]
 
@@ -570,7 +695,7 @@
         for c in range(4):
             at = rows(x, 256 * c)
             FN[at, :] = F[at, :] + L4[at, :] * scale
-    store_f = pltpu.make_async_copy(FN, out_f, l_sem.at[3])
+    store_f = pltpu.make_async_copy(FN, out_f, l_sem.at[13])
     store_f.start()
     T3[...] = zop(FN[pl.ds(512, 256), :], 0)
     for ex in range(2):
@@ -581,10 +706,10 @@
             L1[rows(x), :] = zjoin(-(W[rows(x), :] * div))
     xyjoin(L1)
 
-    ga = ag_start(0, restricted(L1))
     now = faces(L1, 1, 0, *set1, 2)
     pending += now
-    pend_g = list(ga)
+    ga = ag_second(0, ga)
+    pend_g += ga
     finish(now, L1, 1, 0, rx1, ry1, rc1)
     R0[...] = L1[...]
     T1[...] = L1[...] * INVD[...]
@@ -592,10 +717,6 @@
     xyjoin(L1)
     now = faces(L1, 1, 1, *set1, 3)
     pending += now
-    ga = ag_second(0, ga)
-    pend_g += ga
-    ga = ag_third(0, ga)
-    pend_g += ga
     finish(now, L1, 1, 1, rx1, ry1, rc1)
     S0[...] = c1 * T1[...] - c2 * (INVD[...] * L1[...])
     for copy in rowsc:
@@ -636,8 +757,6 @@
     pending += now
     ga = ag_second(1, ga)
     pend_g += ga
-    ga = ag_third(1, ga)
-    pend_g += ga
     finish(now, L1, 1, 3, rx1, ry1, rc1)
     ZI[...] = c1 * T1[...] - c2 * (INVD[...] * L1[...])
     ag_end(1, ga)
@@ -666,9 +785,7 @@
     )
     ga = ag_start(2, row)
     pend_g += ga
-    ga = ag_second(2, ga)
-    pend_g += ga
-    ga = ag_third(2, ga)
+    ga = ag_second(2, ga, True)
     pend_g += ga
     ag_end(2, ga)
     rz1, a11, a10 = sums(2, 3)
@@ -676,7 +793,7 @@
     curv1 = a11 + beta * a10 + beta * beta * curv0
     step1 = rz1 / curv1
     PC[...] = (step0 + step1 * beta) * Z0[...] + step1 * ZI[...]
-    store_p = pltpu.make_async_copy(PC, out_p, l_sem.at[4])
+    store_p = pltpu.make_async_copy(PC, out_p, l_sem.at[14])
     store_p.start()
 
     for copy in pending + side + rowsc + pend_g:
@@ -687,7 +804,7 @@
 
 def per_device(nx, ny, nxc, fields, viscosity, inv_density, elem_group, coarse_inverse):
     nz = nx // nxc
-    cy, bz, cp, spr = constants()
+    cy, bz, cp, spr, fy = constants()
     coarse = coarse_inverse
     if nxc * ny != XC * YL:
         coarse = coarse.reshape(NCD, nz, nxc, ny, NCD)
@@ -700,39 +817,44 @@
 
     field = vm(256, 128)
     scratch = [
+        vm(2, 2, 16), pltpu.VMEM((2, 2, 16), jnp.int32), vm(3, 8, 8, 128),
+        pltpu.VMEM((4, 256, 256), BF16), vm(5, 16, 128), vm(16, 128), vm(36, 16, 128),
+        vm(12, 16, 128), vm(1024, 128), vm(2, 40, 128),
         vm(1024, 128), vm(1024, 128), field, vm(1024, 128), field, field, field,
-        vm(32, 128), field, vm(9, NCD, ncp), vm(8, 128), vm(8, 8, 128), vm(16, 4, 128), field,
+        vm(32, 128), field, vm(9, NCD, ncp), vm(8, 128), vm(8, 8, 128), vm(36, 4, 128), field,
         field, field, field, field, field, field, field, field,
         vm(2, 2, 64, 128), vm(2, 2, 64, 128), vm(2, 4, 4, 128),
         vm(2, 2, 64, 128), vm(2, 2, 64, 128), vm(2, 4, 4, 128),
         vm(4, 2, 16, 128), vm(4, 2, 16, 128), vm(4, 4, 1, 128),
         vm(4, 2, 16, 128), vm(4, 2, 16, 128), vm(4, 4, 1, 128),
-        vm(3, ny, 1, 128), vm(3, nxc, 4, 128), vm(3, nz, 4, 128),
+        vm(3, nxc, ny, 1, 128), vm(3, nz, 4, 128),
         pltpu.SemaphoreType.DMA((6, 8)), pltpu.SemaphoreType.DMA((6, 8)),
         pltpu.SemaphoreType.DMA((8,)), pltpu.SemaphoreType.DMA((8,)),
         pltpu.SemaphoreType.DMA((8,)), pltpu.SemaphoreType.DMA((8,)),
-        pltpu.SemaphoreType.DMA((3, 3, 12)), pltpu.SemaphoreType.DMA((3, 3, 12)),
-        pltpu.SemaphoreType.DMA((5,)),
+        pltpu.SemaphoreType.DMA((3, 76)), pltpu.SemaphoreType.DMA((3, 76)),
+        pltpu.SemaphoreType.DMA((15,)),
     ]
     anywhere = pl.BlockSpec(memory_space=pl.ANY)
-    inside = pl.BlockSpec(memory_space=pltpu.VMEM)
     new, pressure = pl.pallas_call(
         functools.partial(kernel, nx, ny, nxc),
         out_shape=(
             jax.ShapeDtypeStruct((1024, 128), F32),
             jax.ShapeDtypeStruct((256, 128), F32),
         ),
-        in_specs=[anywhere, anywhere, inside, inside, anywhere, inside, inside, inside, inside],
+        in_specs=[pl.BlockSpec(memory_space=pltpu.HBM)] * 10,
         out_specs=(anywhere, anywhere),
         scratch_shapes=scratch,
-        compiler_params=pltpu.CompilerParams(collective_id=0, has_side_effects=True),
+        compiler_params=pltpu.CompilerParams(
+            collective_id=0, has_side_effects=True, vmem_limit_bytes=24 << 20
+        ),
     )(
+        *[pltpu.with_memory_space_constraint(v, pltpu.HBM) for v in (
         fields.reshape(1024, 128),
         viscosity.reshape(256, 128),
         inv_density,
         elem_group,
         coarse,
-        cy, bz, cp, spr,
+        cy, bz, cp, spr, fy)],
     )
     return new.reshape(fields.shape), pressure.reshape(viscosity.shape)
 

time: 83.3 us -> 75 us (0.900)
  Pallas kernels: 79.9 us -> 72.8 us
  local copies, waits for them, and re-layouts: 2.56 us -> 1.45 us
    pallas_call x1, Pallas kernels: 79.9 us -> 72.8 us  [per_device(): pl.pallas_call(functools.partial(kernel, nx, ny, nxc), out_shape=(jax.Sha...]
    unnamed x4 -> x2, local copies, waits for them, and re-layouts: 2.56 us -> 1.45 us
where the time goes in v2:
time: 75 us; the launch traced here: 74.8 us
  Pallas kernels  72.8 us (97%)
  local copies, waits for them, and re-layouts  1.45 us (2%)
    pallas_call x1, Pallas kernels, per_device(): pl.pallas_call(functools.partial(kernel, nx, ny, nxc), out_shape=(jax.Sha...  72.8 us

profile of v2, /device:TPU:1, one launch (start us, length us, event | category | flops | bytes accessed | tf_op | source)
XLA Modules:
  0.0 74.8 jit_solution(11913458299694984749)
XLA Ops:
  0.6 72.8 %shard_map.113 = (f32[1024,128]{1,0:T(8,128)S(1)}, f32[256,128]{1,0:T(8,128)S(1)}) custom-call(f32[1024,128]{1,0:T(8,128)} %bitcast.6, f32[256,128]{1,0:T(8,128)} %bitcast.7, f32[2,2,16]{2,1,0:T(2,128)} %dens_h.1, s32[2,2,16]{2,1,0:T(2,128)} %grp_h.1, f32[4,3072]{1,0:T(4,128)} %coarse.1, f32[3,8,8,128]{3,2,1,0:T(8,128)} %constant.10.clone.cy_h, ...), custom_call_target="tpu_custom_call" | custom-call | tf_op jit(solution)/shard_map/pallas_call | solution.py:838
  73.4 0.8 %copy.14 = f32[4,2,8,2,8,128]{5,4,3,2,1,0:T(8,128)} copy(f32[4,2,8,2,8,128]{5,4,3,2,1,0:T(8,128)S(1)} %bitcast.4) | data formatting | bytes 1048576
  74.2 0.7 copy.15

commit v3 on v2

--- a/solution.py
+++ b/solution.py
@@ -186,15 +186,6 @@
     def p_mate(dx, dy):
         return (zc * nxc + (xc + dx) % nxc, (gy + dy) % ny)
 
-    mates = [nbr(dx, dy) for dx, dy in DIRS if dx != 0]
-    mates += [p_mate(*off) for off in flat]
-    mates += [z_mate(k) for k in zline]
-    if nxc * ny < 4:
-        mates += [nbr(0, -1), nbr(0, 1)]
-    barrier = pltpu.get_barrier_semaphore()
-    for mate in mates:
-        pl.semaphore_signal(barrier, inc=1, device_id=mate, device_id_type=MESH)
-
     load_f = []
     for c in range(4):
         part = pl.ds(256 * c, 256)
@@ -211,6 +202,15 @@
     for copy in load_f + load_s + load_l + [load_c]:
         copy.start()
 
+    ranked = [(hops(off), p_mate(*off)) for off in flat]
+    ranked += [(min(k, nz - k), z_mate(k)) for k in zline]
+    ranked += [(2 + abs(dy), nbr(dx, dy)) for dx, dy in DIRS if dx != 0 or nxc * ny < 4]
+    ranked.sort(key=lambda item: -item[0])
+    mates = [mate for _, mate in ranked]
+    barrier = pltpu.get_barrier_semaphore()
+    for mate in mates:
+        pl.semaphore_signal(barrier, inc=1, device_id=mate, device_id_type=MESH)
+
     lane = lax.broadcasted_iota(jnp.int32, (8, 128), 1)
     sub = lax.broadcasted_iota(jnp.int32, (8, 128), 0)
     one = jnp.float32(1.0)
@@ -254,12 +254,20 @@
             parts.append(total)
         return jnp.concatenate(parts, 0)
 
-    def xop(planes, coef):
-        total = None
-        for a in range(8):
-            term = planes[a] * jnp.float32(coef[a])
-            total = term if total is None else total + term
-        return total
+    def xop(planes, matrix, sign):
+        even = [planes[a] + planes[7 - a] for a in range(4)]
+        odd = [planes[a] - planes[7 - a] for a in range(4)]
+        out = [None] * 8
+        for i in range(4):
+            p = q = None
+            for a in range(4):
+                both = even[a] * jnp.float32((matrix[i, a] + matrix[i, 7 - a]) / 2)
+                diff = odd[a] * jnp.float32((matrix[i, a] - matrix[i, 7 - a]) / 2)
+                p = both if p is None else p + both
+                q = diff if q is None else q + diff
+            out[i] = p + q
+            out[7 - i] = p - q if sign > 0 else q - p
+        return out
 
     def zop(f, which):
         high = f.astype(BF16)
@@ -268,9 +276,10 @@
         prod = jnp.dot(both, bz[which], preferred_element_type=F32)
         return prod[:, :128] + prod[:, 128:]
 
-    def faces(L, nch, e, sx, sy, sc, rx, ry, rc, num):
+    def faces(L, nch, e, sx, sy, sc, rx, ry, rc, num, start=0):
+        used = pl.ds(0, 16 * nch)
         for c in range(nch):
-            base = 256 * c
+            base = start + 256 * c
             sx[e, 0, pl.ds(16 * c, 16), :] = L[pl.ds(base, 16), :]
             sx[e, 1, pl.ds(16 * c, 16), :] = L[pl.ds(base + 240, 16), :]
             sy[e, 0, pl.ds(16 * c, 16), :] = L[pl.ds(base, 16, stride=16), :]
@@ -281,9 +290,9 @@
         copies = []
         for d in (4, 5, 6, 7, 0, 1, 2, 3):
             if d < 2:
-                src, dst = sx.at[e, d], rx.at[e, d]
+                src, dst = sx.at[e, d, used], rx.at[e, d, used]
             elif d < 4:
-                src, dst = sy.at[e, d - 2], ry.at[e, d - 2]
+                src, dst = sy.at[e, d - 2, used], ry.at[e, d - 2, used]
             else:
                 src, dst = sc.at[e, d - 4], rc.at[e, d - 4]
             copy = pltpu.make_async_remote_copy(
@@ -294,11 +303,11 @@
             copies.append(copy)
         return copies
 
-    def finish(copies, L, nch, e, rx, ry, rc):
+    def finish(copies, L, nch, e, rx, ry, rc, start=0):
         for copy in copies:
             copy.wait_recv()
         for c in range(nch):
-            base = 256 * c
+            base = start + 256 * c
             at = pl.ds(16 * c, 16)
             lo, hi = pl.ds(base, 16), pl.ds(base + 240, 16)
             L[lo, :] = L[lo, :] + has_l * rx[e, 1, at, :]
@@ -407,14 +416,17 @@
         OH[6 * ex + ey] = jnp.where(hit, valid, zero)
 
     def channel(c, carry):
-        base = pl.multiple_of(c * 256, 256)
-        coef = jnp.where(c == 3, jnp.float32(1.0 / prandtl), one)
+        if isinstance(c, int):
+            base, coef = c * 256, jnp.float32(1.0 / prandtl)
+        else:
+            base, coef = pl.multiple_of(c * 256, 256), one
         T3[...] = zop(F[pl.ds(base, 256), :], 0)
         for ex in range(2):
             planes = [F[pl.ds(base + 16 * (8 * ex + a), 16), :] for a in range(8)]
+            slopes = xop(planes, DER, -1)
             for i in range(8):
                 x = 8 * ex + i
-                gxp = xop(planes, DER[i])
+                gxp = slopes[i]
                 gyp = yop(planes[i], 0)
                 gzp = T3[rows(x), :]
                 adv = (
@@ -426,18 +438,21 @@
                 T3[rows(x), :] = nuw * gzp
         T3[...] = zop(T3[...], 1) + T2[...]
         for ex in range(2):
-            planes = [T1[rows(8 * ex + a), :] for a in range(8)]
+            turned = xop([T1[rows(8 * ex + a), :] for a in range(8)], DER.T, -1)
             for i in range(8):
                 x = 8 * ex + i
-                total = xop(planes, DER[:, i]) + T3[rows(x), :]
+                total = turned[i] + T3[rows(x), :]
                 at = pl.ds(base + 16 * x, 16)
-                G[at, :] = W[rows(x), :] * F[at, :] - jnp.float32(dt_step) * total
+                if not isinstance(c, int):
+                    G[at, :] = W[rows(x), :] * F[at, :] - jnp.float32(dt_step) * total
                 L4[at, :] = zjoin(-total)
         xyjoin(L4, base)
         return carry
 
-    lax.fori_loop(0, 4, channel, 0)
-    now = faces(L4, 4, 1, *set4, 1)
+    lax.fori_loop(0, 3, channel, 0)
+    for k in range(4):
+        sc4[1, k, pl.ds(3, 1), :] = jnp.zeros((1, 128), F32)
+    now = faces(L4, 3, 1, *set4, 1)
     pending += now
 
     group = lane[0:1] // 32
@@ -609,6 +624,9 @@
 
     ga = ag_start(0, restricted_early())
     pend_g = list(ga)
+    channel(3, 0)
+    warm = faces(L4, 1, 4, *set1, 6, start=768)
+    pending += warm
 
     xsets = [(0, 1), (1,), (1, 2), (2,), (2, 3)]
     xclass = [0] + [1] * 6 + [2, 2] + [3] * 6 + [4]
@@ -667,11 +685,12 @@
         T3[...] = zop(q[...], 2)
         for ex in range(2):
             planes = [q[rows(8 * ex + a), :] for a in range(8)]
+            stiff = xop(planes, STF, 1)
             kap = KAP[pl.ds(16 * ex, 16), :]
             for i in range(8):
                 x = 8 * ex + i
                 wa = jnp.float32(WTS[i])
-                kx = xop(planes, STF[i])
+                kx = stiff[i]
                 ky = yop(planes[i], 2)
                 inner = cp[0] * kx + wa * (cp[1] * ky + cp[2] * T3[rows(x), :])
                 put(x, planes[i], kap * inner + (jnp.float32(sigma_p) * wa) * (cp[0] * planes[i]))
@@ -689,20 +708,21 @@
     c1 = jnp.float32((1.0 + rho_next * rho) / theta + c2)
     c2 = jnp.float32(c2 / theta)
 
-    finish(now, L4, 4, 1, rx4, ry4, rc4)
-    for x in range(16):
-        scale = (jnp.float32(dt_step / WTS[x % 8]) * imx[x]) * (imyz * cp[4])
-        for c in range(4):
-            at = rows(x, 256 * c)
-            FN[at, :] = F[at, :] + L4[at, :] * scale
-    store_f = pltpu.make_async_copy(FN, out_f, l_sem.at[13])
-    store_f.start()
+    def renew(channels):
+        for x in range(16):
+            scale = (jnp.float32(dt_step / WTS[x % 8]) * imx[x]) * (imyz * cp[4])
+            for c in channels:
+                at = rows(x, 256 * c)
+                FN[at, :] = F[at, :] + L4[at, :] * scale
+
+    finish(now, L4, 3, 1, rx4, ry4, rc4)
+    renew(range(3))
     T3[...] = zop(FN[pl.ds(512, 256), :], 0)
     for ex in range(2):
-        planes = [FN[rows(8 * ex + a), :] for a in range(8)]
+        slopes = xop([FN[rows(8 * ex + a), :] for a in range(8)], DER, -1)
         for i in range(8):
             x = 8 * ex + i
-            div = xop(planes, DER[i]) + yop(FN[rows(x, 256), :], 0) + T3[rows(x), :]
+            div = slopes[i] + yop(FN[rows(x, 256), :], 0) + T3[rows(x), :]
             L1[rows(x), :] = zjoin(-(W[rows(x), :] * div))
     xyjoin(L1)
 
@@ -717,6 +737,10 @@
     xyjoin(L1)
     now = faces(L1, 1, 1, *set1, 3)
     pending += now
+    finish(warm, L4, 1, 4, rx1, ry1, rc1, start=768)
+    renew([3])
+    store_f = pltpu.make_async_copy(FN, out_f, l_sem.at[13])
+    store_f.start()
     finish(now, L1, 1, 1, rx1, ry1, rc1)
     S0[...] = c1 * T1[...] - c2 * (INVD[...] * L1[...])
     for copy in rowsc:
@@ -784,9 +808,14 @@
         jnp.zeros((1, 128), F32), [full(rz_part * imyz), full(dots[0]), full(dots[1])]
     )
     ga = ag_start(2, row)
-    pend_g += ga
+    for copy in pending + side + rowsc + pend_g:
+        copy.wait_send()
+    store_f.wait()
+    for copy in ga:
+        copy.wait_send()
     ga = ag_second(2, ga, True)
-    pend_g += ga
+    for copy in ga:
+        copy.wait_send()
     ag_end(2, ga)
     rz1, a11, a10 = sums(2, 3)
     beta = rz1 / rz0
@@ -796,9 +825,6 @@
     store_p = pltpu.make_async_copy(PC, out_p, l_sem.at[14])
     store_p.start()
 
-    for copy in pending + side + rowsc + pend_g:
-        copy.wait_send()
-    store_f.wait()
     store_p.wait()
 
 
@@ -825,10 +851,10 @@
         field, field, field, field, field, field, field, field,
         vm(2, 2, 64, 128), vm(2, 2, 64, 128), vm(2, 4, 4, 128),
         vm(2, 2, 64, 128), vm(2, 2, 64, 128), vm(2, 4, 4, 128),
-        vm(4, 2, 16, 128), vm(4, 2, 16, 128), vm(4, 4, 1, 128),
-        vm(4, 2, 16, 128), vm(4, 2, 16, 128), vm(4, 4, 1, 128),
+        vm(5, 2, 16, 128), vm(5, 2, 16, 128), vm(5, 4, 1, 128),
+        vm(5, 2, 16, 128), vm(5, 2, 16, 128), vm(5, 4, 1, 128),
         vm(3, nxc, ny, 1, 128), vm(3, nz, 4, 128),
-        pltpu.SemaphoreType.DMA((6, 8)), pltpu.SemaphoreType.DMA((6, 8)),
+        pltpu.SemaphoreType.DMA((7, 8)), pltpu.SemaphoreType.DMA((7, 8)),
         pltpu.SemaphoreType.DMA((8,)), pltpu.SemaphoreType.DMA((8,)),
         pltpu.SemaphoreType.DMA((8,)), pltpu.SemaphoreType.DMA((8,)),
         pltpu.SemaphoreType.DMA((3, 76)), pltpu.SemaphoreType.DMA((3, 76)),

time: 75 us -> 73.7 us (0.983)
  Pallas kernels: 72.8 us -> 71.4 us
    pallas_call x1, Pallas kernels: 72.8 us -> 71.4 us  [per_device(): pl.pallas_call(functools.partial(kernel, nx, ny, nxc), out_shape=(jax.Sha...]
where the time goes in v3:
time: 73.7 us; the launch traced here: 73.5 us
  Pallas kernels  71.4 us (97%)
  local copies, waits for them, and re-layouts  1.45 us (2%)
    pallas_call x1, Pallas kernels, per_device(): pl.pallas_call(functools.partial(kernel, nx, ny, nxc), out_shape=(jax.Sha...  71.4 us

profile of v3, /device:TPU:1, one launch (start us, length us, event | category | flops | bytes accessed | tf_op | source)
XLA Modules:
  0.0 73.5 jit_solution(12217580259623382590)
XLA Ops:
  0.6 71.4 %shard_map.113 = (f32[1024,128]{1,0:T(8,128)S(1)}, f32[256,128]{1,0:T(8,128)S(1)}) custom-call(f32[1024,128]{1,0:T(8,128)} %bitcast.6, f32[256,128]{1,0:T(8,128)} %bitcast.7, f32[2,2,16]{2,1,0:T(2,128)} %dens_h.1, s32[2,2,16]{2,1,0:T(2,128)} %grp_h.1, f32[4,3072]{1,0:T(4,128)} %coarse.1, f32[3,8,8,128]{3,2,1,0:T(8,128)} %constant.10.clone.cy_h, ...), custom_call_target="tpu_custom_call" | custom-call | tf_op jit(solution)/shard_map/pallas_call | solution.py:864
  72.1 0.8 %copy.14 = f32[4,2,8,2,8,128]{5,4,3,2,1,0:T(8,128)} copy(f32[4,2,8,2,8,128]{5,4,3,2,1,0:T(8,128)S(1)} %bitcast.4) | data formatting | bytes 1048576
  72.9 0.7 copy.15

commit v4 on v3

--- a/solution.py
+++ b/solution.py
@@ -155,7 +155,7 @@
     nx, ny, nxc,
     fields, visc, dens_h, grp_h, coarse, cy_h, bz_h, cp_h, spr_h, fy_h,
     out_f, out_p,
-    dens, grp, cy, bz, cp, spr, fy, YF, G, TR,
+    dens, grp, cy, bz, cp, spr, fy, YF, G, TR, C1, C2, C3, C4, W2,
     F, FN, V, L4, L1, W, IM, KAP, INVD, CX, AUX, AUXR, OH, PC,
     T1, T2, T3, R0, S0, Z0, W1, ZI,
     sx4, sy4, sc4, rx4, ry4, rc4, sx1, sy1, sc1, rx1, ry1, rc1,
@@ -415,41 +415,44 @@
         hit = jnp.abs(jnp.broadcast_to(grow, (4, 128)) - sub[0:4].astype(F32)) < half
         OH[6 * ex + ey] = jnp.where(hit, valid, zero)
 
-    def channel(c, carry):
-        if isinstance(c, int):
-            base, coef = c * 256, jnp.float32(1.0 / prandtl)
-        else:
-            base, coef = pl.multiple_of(c * 256, 256), one
-        T3[...] = zop(F[pl.ds(base, 256), :], 0)
-        for ex in range(2):
-            planes = [F[pl.ds(base + 16 * (8 * ex + a), 16), :] for a in range(8)]
-            slopes = xop(planes, DER, -1)
-            for i in range(8):
-                x = 8 * ex + i
-                gxp = slopes[i]
-                gyp = yop(planes[i], 0)
-                gzp = T3[rows(x), :]
-                adv = (
-                    F[rows(x), :] * gxp + F[rows(x, 256), :] * gyp + F[rows(x, 512), :] * gzp
-                )
-                nuw = coef * V[rows(x), :]
-                T1[rows(x), :] = nuw * gxp
-                T2[rows(x), :] = yop(nuw * gyp, 1) + W[rows(x), :] * adv
-                T3[rows(x), :] = nuw * gzp
-        T3[...] = zop(T3[...], 1) + T2[...]
-        for ex in range(2):
-            turned = xop([T1[rows(8 * ex + a), :] for a in range(8)], DER.T, -1)
-            for i in range(8):
-                x = 8 * ex + i
-                total = turned[i] + T3[rows(x), :]
-                at = pl.ds(base + 16 * x, 16)
-                if not isinstance(c, int):
-                    G[at, :] = W[rows(x), :] * F[at, :] - jnp.float32(dt_step) * total
-                L4[at, :] = zjoin(-total)
-        xyjoin(L4, base)
-        return carry
-
-    lax.fori_loop(0, 3, channel, 0)
+    def channels(which):
+        for c in which:
+            at = pl.ds(256 * c, 256)
+            C3[at, :] = zop(F[at, :], 0)
+        for c in which:
+            base = 256 * c
+            coef = None if c < 3 else jnp.float32(1.0 / prandtl)
+            for ex in range(2):
+                planes = [F[rows(8 * ex + a, base), :] for a in range(8)]
+                slopes = xop(planes, DER, -1)
+                for i in range(8):
+                    x = 8 * ex + i
+                    gxp = slopes[i]
+                    gyp = yop(planes[i], 0)
+                    gzp = C3[rows(x, base), :]
+                    adv = (
+                        F[rows(x), :] * gxp + F[rows(x, 256), :] * gyp + F[rows(x, 512), :] * gzp
+                    )
+                    nuw = V[rows(x), :] if coef is None else coef * V[rows(x), :]
+                    C1[rows(x, base), :] = nuw * gxp
+                    C2[rows(x, base), :] = yop(nuw * gyp, 1) + W[rows(x), :] * adv
+                    C4[rows(x, base), :] = nuw * gzp
+            at = pl.ds(base, 256)
+            C3[at, :] = zop(C4[at, :], 1)
+        for c in which:
+            base = 256 * c
+            for ex in range(2):
+                turned = xop([C1[rows(8 * ex + a, base), :] for a in range(8)], DER.T, -1)
+                for i in range(8):
+                    x = 8 * ex + i
+                    at = rows(x, base)
+                    total = turned[i] + (C3[at, :] + C2[at, :])
+                    if c < 3:
+                        G[at, :] = W[rows(x), :] * F[at, :] - jnp.float32(dt_step) * total
+                    L4[at, :] = zjoin(-total)
+            xyjoin(L4, base)
+
+    channels(range(3))
     for k in range(4):
         sc4[1, k, pl.ds(3, 1), :] = jnp.zeros((1, 128), F32)
     now = faces(L4, 3, 1, *set4, 1)
@@ -624,7 +627,7 @@
 
     ga = ag_start(0, restricted_early())
     pend_g = list(ga)
-    channel(3, 0)
+    channels([3])
     warm = faces(L4, 1, 4, *set1, 6, start=768)
     pending += warm
 
@@ -679,7 +682,8 @@
                 value = values[slot_of(dx, dy)]
                 line.append(jnp.sum(OH[6 * ex + ey + 7] * value, axis=0, keepdims=True))
             grid.append(line)
-        return [plane * imyz for plane in spread(grid)]
+        planes = [plane * imyz for plane in spread(grid)]
+        return [imx[0] * planes[0], planes[1], half * planes[2], planes[3], imx[15] * planes[4]]
 
     def apply_local(q, put):
         T3[...] = zop(q[...], 2)
@@ -694,6 +698,27 @@
                 ky = yop(planes[i], 2)
                 inner = cp[0] * kx + wa * (cp[1] * ky + cp[2] * T3[rows(x), :])
                 put(x, planes[i], kap * inner + (jnp.float32(sigma_p) * wa) * (cp[0] * planes[i]))
+
+    def apply_coarse(values):
+        flat_z = zop(jnp.concatenate(values, 0), 2)
+        rest = [
+            cp[1] * yop(values[k], 2) + cp[2] * flat_z[16 * k : 16 * k + 16] for k in range(5)
+        ]
+        scaled = [cp[0] * values[k] for k in range(5)]
+        out = []
+        for ex in range(2):
+            kap = KAP[pl.ds(16 * ex, 16), :]
+            low, mid, high = scaled[2 * ex], scaled[2 * ex + 1], scaled[2 * ex + 2]
+            for i in range(8):
+                wa = jnp.float32(WTS[i])
+                k = xclass[8 * ex + i]
+                kx = (
+                    jnp.float32(STF[i, 0]) * low
+                    + jnp.float32(np.sum(STF[i, 1:7])) * mid
+                    + jnp.float32(STF[i, 7]) * high
+                )
+                out.append(kap * (kx + wa * rest[k]) + (jnp.float32(sigma_p) * wa) * scaled[k])
+        return out
 
     def put_joined(x, plane, value):
         L1[rows(x), :] = zjoin(value)
@@ -743,31 +768,35 @@
     store_f.start()
     finish(now, L1, 1, 1, rx1, ry1, rc1)
     S0[...] = c1 * T1[...] - c2 * (INVD[...] * L1[...])
+
+    def put_smooth(x, plane, value):
+        W1[rows(x), :] = value
+
+    apply_local(S0, put_smooth)
     for copy in rowsc:
         copy.wait_recv()
     ag_end(0, ga)
-    planes = coarse_planes(0)
+    values = coarse_planes(0)
+
+    images = apply_coarse(values)
+    dot = rz_part = None
     for x in range(16):
-        Z0[rows(x), :] = S0[rows(x), :] + imx[x] * planes[xclass[x]]
-
-    dot = []
-
-    def put_first(x, plane, value):
-        W1[rows(x), :] = value
-        L1[rows(x), :] = zjoin(value)
-        term = plane * value
-        dot.append(term if not dot else dot.pop() + term)
+        at = rows(x)
+        z0 = S0[at, :] + values[xclass[x]]
+        value = W1[at, :] + images[x]
+        Z0[at, :] = z0
+        W1[at, :] = value
+        L1[at, :] = zjoin(value)
+        term = z0 * value
+        dot = term if dot is None else dot + term
+        term = imx[x] * (R0[at, :] * z0)
+        rz_part = term if rz_part is None else rz_part + term
 
     def full(v):
         return jnp.sum(jnp.sum(v, axis=0, keepdims=True), axis=1, keepdims=True)
 
-    apply_local(Z0, put_first)
     xyjoin(L1)
-    rz_part = None
-    for x in range(16):
-        term = imx[x] * (R0[rows(x), :] * Z0[rows(x), :])
-        rz_part = term if rz_part is None else rz_part + term
-    row = with_sums(restricted(L1), [full(rz_part * imyz), full(dot.pop())])
+    row = with_sums(restricted(L1), [full(rz_part * imyz), full(dot)])
     ga = ag_start(1, row)
     pend_g += ga
     now = faces(L1, 1, 2, *set1, 4)
@@ -783,27 +812,32 @@
     pend_g += ga
     finish(now, L1, 1, 3, rx1, ry1, rc1)
     ZI[...] = c1 * T1[...] - c2 * (INVD[...] * L1[...])
+
+    def put_second(x, plane, value):
+        W2[rows(x), :] = value
+
+    apply_local(ZI, put_second)
     ag_end(1, ga)
     rz0, curv0 = sums(1, 2)
     step0 = rz0 / curv0
-    planes = coarse_planes(1)
+    values = coarse_planes(1)
+
+    images = apply_coarse(values)
     rz_part = None
+    dots = [None, None]
     for x in range(16):
         at = rows(x)
-        zi = ZI[at, :] + imx[x] * planes[xclass[x]]
-        z1 = Z0[at, :] - step0 * zi
+        z0 = Z0[at, :]
+        first = W1[at, :]
+        z1 = z0 - step0 * (ZI[at, :] + values[xclass[x]])
+        second = first - step0 * (W2[at, :] + images[x])
         ZI[at, :] = z1
         term = imx[x] * ((R0[at, :] - step0 * T2[at, :]) * z1)
         rz_part = term if rz_part is None else rz_part + term
-
-    dots = [None, None]
-
-    def put_second(x, plane, value):
-        terms = (plane * value, Z0[rows(x), :] * value + plane * W1[rows(x), :])
+        terms = (z1 * second, z0 * second + z1 * first)
         for k in range(2):
             dots[k] = terms[k] if dots[k] is None else dots[k] + terms[k]
 
-    apply_local(ZI, put_second)
     row = with_sums(
         jnp.zeros((1, 128), F32), [full(rz_part * imyz), full(dots[0]), full(dots[1])]
     )
@@ -846,6 +880,7 @@
         vm(2, 2, 16), pltpu.VMEM((2, 2, 16), jnp.int32), vm(3, 8, 8, 128),
         pltpu.VMEM((4, 256, 256), BF16), vm(5, 16, 128), vm(16, 128), vm(36, 16, 128),
         vm(12, 16, 128), vm(1024, 128), vm(2, 40, 128),
+        vm(1024, 128), vm(1024, 128), vm(1024, 128), vm(1024, 128), field,
         vm(1024, 128), vm(1024, 128), field, vm(1024, 128), field, field, field,
         vm(32, 128), field, vm(9, NCD, ncp), vm(8, 128), vm(8, 8, 128), vm(36, 4, 128), field,
         field, field, field, field, field, field, field, field,

time: 73.7 us -> 73.5 us (level)
  no operation moved by 1% of the time
where the time goes in v4:
time: 73.5 us; the launch traced here: 73.3 us
  Pallas kernels  71.2 us (97%)
  local copies, waits for them, and re-layouts  1.45 us (2%)
    pallas_call x1, Pallas kernels, per_device(): pl.pallas_call(functools.partial(kernel, nx, ny, nxc), out_shape=(jax.Sha...  71.2 us

profile of v4, /device:TPU:1, one launch (start us, length us, event | category | flops | bytes accessed | tf_op | source)
XLA Modules:
  0.0 73.3 jit_solution(13614322940189561931)
XLA Ops:
  0.6 71.2 %shard_map.113 = (f32[1024,128]{1,0:T(8,128)S(1)}, f32[256,128]{1,0:T(8,128)S(1)}) custom-call(f32[1024,128]{1,0:T(8,128)} %bitcast.6, f32[256,128]{1,0:T(8,128)} %bitcast.7, f32[2,2,16]{2,1,0:T(2,128)} %dens_h.1, s32[2,2,16]{2,1,0:T(2,128)} %grp_h.1, f32[4,3072]{1,0:T(4,128)} %coarse.1, f32[3,8,8,128]{3,2,1,0:T(8,128)} %constant.10.clone.cy_h, ...), custom_call_target="tpu_custom_call" | custom-call | tf_op jit(solution)/shard_map/pallas_call | solution.py:899
  71.9 0.8 %copy.14 = f32[4,2,8,2,8,128]{5,4,3,2,1,0:T(8,128)} copy(f32[4,2,8,2,8,128]{5,4,3,2,1,0:T(8,128)S(1)} %bitcast.4) | data formatting | bytes 1048576
  72.7 0.7 copy.15

commit v5 on v4

--- a/solution.py
+++ b/solution.py
@@ -323,14 +323,23 @@
     set1 = (sx1, sy1, sc1, rx1, ry1, rc1)
     pending = []
 
-    for c in range(4):
+    def joined(c):
         load_f[c].wait()
         for x in range(16):
             L4[rows(x, 256 * c), :] = zjoin(F[rows(x, 256 * c), :])
         xyjoin(L4, 256 * c)
+
+    for c in range(3):
+        joined(c)
+    for e in range(2):
+        for k in range(4):
+            sc4[e, k, pl.ds(3, 1), :] = jnp.zeros((1, 128), F32)
     pl.semaphore_wait(barrier, len(mates))
-    now = faces(L4, 4, 0, *set4, 0)
+    now = faces(L4, 3, 0, *set4, 0)
     pending += now
+    joined(3)
+    heat = faces(L4, 1, 5, *set1, 7, start=768)
+    pending += heat
     for copy in load_s:
         copy.wait()
     for ex in range(2):
@@ -382,8 +391,8 @@
     no_b, no_t = one - has_b, one - has_t
     for k in range(12):
         YF[k] = fy[k] + no_b * fy[12 + k] + no_t * fy[24 + k]
-    finish(now, L4, 4, 0, rx4, ry4, rc4)
-    for c in range(4):
+    finish(now, L4, 3, 0, rx4, ry4, rc4)
+    for c in range(3):
         at = pl.ds(256 * c, 256)
         F[at, :] = L4[at, :] * IM[...]
 
@@ -453,8 +462,6 @@
             xyjoin(L4, base)
 
     channels(range(3))
-    for k in range(4):
-        sc4[1, k, pl.ds(3, 1), :] = jnp.zeros((1, 128), F32)
     now = faces(L4, 3, 1, *set4, 1)
     pending += now
 
@@ -627,6 +634,8 @@
 
     ga = ag_start(0, restricted_early())
     pend_g = list(ga)
+    finish(heat, L4, 1, 5, rx1, ry1, rc1, start=768)
+    F[pl.ds(768, 256), :] = L4[pl.ds(768, 256), :] * IM[...]
     channels([3])
     warm = faces(L4, 1, 4, *set1, 6, start=768)
     pending += warm
@@ -862,6 +871,15 @@
     store_p.wait()
 
 
+def place(new, pressure, out_f, out_p, sems):
+    first = pltpu.make_async_copy(new, out_f, sems.at[0])
+    second = pltpu.make_async_copy(pressure, out_p, sems.at[1])
+    first.start()
+    second.start()
+    first.wait()
+    second.wait()
+
+
 def per_device(nx, ny, nxc, fields, viscosity, inv_density, elem_group, coarse_inverse):
     nz = nx // nxc
     cy, bz, cp, spr, fy = constants()
@@ -886,10 +904,10 @@
         field, field, field, field, field, field, field, field,
         vm(2, 2, 64, 128), vm(2, 2, 64, 128), vm(2, 4, 4, 128),
         vm(2, 2, 64, 128), vm(2, 2, 64, 128), vm(2, 4, 4, 128),
-        vm(5, 2, 16, 128), vm(5, 2, 16, 128), vm(5, 4, 1, 128),
-        vm(5, 2, 16, 128), vm(5, 2, 16, 128), vm(5, 4, 1, 128),
+        vm(6, 2, 16, 128), vm(6, 2, 16, 128), vm(6, 4, 1, 128),
+        vm(6, 2, 16, 128), vm(6, 2, 16, 128), vm(6, 4, 1, 128),
         vm(3, nxc, ny, 1, 128), vm(3, nz, 4, 128),
-        pltpu.SemaphoreType.DMA((7, 8)), pltpu.SemaphoreType.DMA((7, 8)),
+        pltpu.SemaphoreType.DMA((8, 8)), pltpu.SemaphoreType.DMA((8, 8)),
         pltpu.SemaphoreType.DMA((8,)), pltpu.SemaphoreType.DMA((8,)),
         pltpu.SemaphoreType.DMA((8,)), pltpu.SemaphoreType.DMA((8,)),
         pltpu.SemaphoreType.DMA((3, 76)), pltpu.SemaphoreType.DMA((3, 76)),
@@ -917,6 +935,17 @@
         coarse,
         cy, bz, cp, spr, fy)],
     )
+    new, pressure = pl.pallas_call(
+        place,
+        out_shape=(
+            jax.ShapeDtypeStruct((1024, 128), F32),
+            jax.ShapeDtypeStruct((256, 128), F32),
+        ),
+        in_specs=[anywhere] * 2,
+        out_specs=(pl.BlockSpec(memory_space=pltpu.HBM),) * 2,
+        scratch_shapes=[pltpu.SemaphoreType.DMA((2,))],
+        compiler_params=pltpu.CompilerParams(vmem_limit_bytes=4 << 20),
+    )(new, pressure)
     return new.reshape(fields.shape), pressure.reshape(viscosity.shape)
 
 

time: 73.5 us -> 73 us (level)
  local copies, waits for them, and re-layouts: 1.45 us -> 0 us
  Pallas kernels: 71.2 us -> 72.3 us
    unnamed x2 -> x0, local copies, waits for them, and re-layouts: 1.45 us -> none
    pallas_call x0 -> x1, Pallas kernels: none -> 0.85 us  [per_device(): pl.pallas_call(place, out_shape=(jax.ShapeDtypeStruct((1024, 128), F32),...]
where the time goes in v5:
time: 73 us; the launch traced here: 72.9 us
  Pallas kernels  72.3 us (99%)
    pallas_call x1, Pallas kernels, per_device(): pl.pallas_call(functools.partial(kernel, nx, ny, nxc), out_shape=(jax.Sha...  71.4 us

profile of v5, /device:TPU:1, one launch (start us, length us, event | category | flops | bytes accessed | tf_op | source)
XLA Modules:
  0.0 72.9 jit_solution(9995362984979993238)
XLA Ops:
  0.6 71.4 %shard_map.113 = (f32[1024,128]{1,0:T(8,128)S(1)}, f32[256,128]{1,0:T(8,128)S(1)}) custom-call(f32[1024,128]{1,0:T(8,128)} %bitcast.4, f32[256,128]{1,0:T(8,128)} %bitcast.5, f32[2,2,16]{2,1,0:T(2,128)} %dens_h.1, s32[2,2,16]{2,1,0:T(2,128)} %grp_h.1, f32[4,3072]{1,0:T(4,128)} %coarse.1, f32[3,8,8,128]{3,2,1,0:T(8,128)} %constant.10.clone.cy_h, ...), custom_call_target="tpu_custom_call" | custom-call | tf_op jit(solution)/shard_map/pallas_call | solution.py:917
  72.0 0.8 %shard_map.114 = (f32[1024,128]{1,0:T(8,128)}, f32[256,128]{1,0:T(8,128)}) custom-call(f32[1024,128]{1,0:T(8,128)S(1)} %get-tuple-element.6.new, f32[256,128]{1,0:T(8,128)S(1)} %get-tuple-element.7.pressure), custom_call_target="tpu_custom_call" | custom-call | tf_op jit(solution)/shard_map/pallas_call | solution.py:938
